TPU v7x, 32 devices: a whole 2x2x4 slice. The times are simulated.
32 devices in a mesh: slab: 4 (over x, core), space: 8 (over z, y).
Axes of the slice: x: 2, y: 2, z: 4, core: 2. Of those that a mesh axis runs over, the one named last changes fastest.
Arguments:
- forcing: float32 [8, 3, 4, 4, 4, 8192], P('slab', None, None, None, None, 'space'), may hold values from -6 to 6
- coefficient: float32 [8192], P('space'), may hold values from 1.5 to 4
- neighbours: int32 [6, 8192], P(None, 'space'), may hold values from 0 to 2048, as said below
- halo_faces: int32 [2, 4096], P(None, 'space'), may hold values from 0 to 1023, as said below
- time_block: float32 [3, 3], replicated, may hold values from -0.6 to 1.6
- space_block: float32 [4, 4], replicated, may hold values from -0.6 to 1.6
- stiffness: float32 [4, 4], replicated, may hold values from -0.6 to 0.6
- time_restrict: float32 [1, 3], replicated, may hold values from 0.5 to 1.5
- space_restrict: float32 [2, 4], replicated, may hold values from 0.5 to 1.5
- coarse_smoother: float32 [2, 2], replicated, may hold values from -0.8 to 1.8
Outputs:
- correction: float32 [8, 3, 4, 4, 4, 8192], P('slab', None, None, None, None, 'space')
Inputs may be any that keep to these rules, and one draw needn't show every extreme that they name: `neighbours`: for element e of partition p (local numbers below 1024) and face f = -x, +x, -y, +y, -z, +z in that order: a local element of p whose opposite face is the same face with the same node order, or 1024 + m for the m-th element of the left partition's rightward list (row 1 of halo_faces), or 1536 + m for the m-th element of the right partition's leftward list (row 0), or 2048 where the face lies on the domain boundary. Ghost slots appear only for the -x face (left) and the +x face (right). `halo_faces`: row 0 lists, in local numbers, the 512 elements of a partition whose -x face touches the left partition, row 1 those whose +x face touches the right partition, each once.
All inputs are finite; a program needn't handle non-finite values.
Results may differ from a plain program's by a relative error of at most 0.00027.
Values sent between devices are 32-bit elements; how exact they have to be, the bound alone decides.
No kernel may reach another device: no remote copies, remote signals or barrier semaphores. Data moves between devices by JAX's collectives and lax.ppermute only.
A program may use at most 128 MiB of HBM per device.

v0:
```python
import functools

import jax
import jax.numpy as jnp
from jax import lax
from jax.experimental import pallas as pl
from jax.experimental.pallas import tpu as pltpu
from jax.sharding import PartitionSpec as P

SWEEPS = 3
PENALTY = 0.3
UPWIND = 0.5
COARSE_UPWIND = 0.6
F32 = jnp.float32
BF16 = jnp.bfloat16
VMEM_BYTES = 56 * 1024 * 1024


def exact(a, b):
    return jnp.dot(a, b, precision=lax.Precision.HIGHEST, preferred_element_type=F32)


def iota(shape, dim):
    return lax.broadcasted_iota(jnp.int32, shape, dim)


def expand(small, rows, row_digit, cols, col_digit):
    n, m = small.shape
    left = (row_digit(iota((rows, n), 0)) == iota((rows, n), 1)).astype(F32)
    right = (iota((m, cols), 0) == col_digit(iota((m, cols), 1))).astype(F32)
    return exact(exact(left, small), right)


class Nodes:
    def __init__(self, q, p, pc):
        self.q, self.p, self.pc = q, p, pc
        self.n = q * p**3
        self.nc = pc**3
        self.nf = 6 * pc**2

    def fine(self, d):
        p = self.p
        if d == 0:
            return lambda r: r // p**3
        return lambda r: (r // p ** (3 - d)) % p

    def coarse(self, d):
        pc = self.pc
        return lambda r: (r // pc ** (3 - d)) % pc

    def face(self, r):
        return r // self.pc**2

    def bit(self, d, r):
        pc = self.pc
        high, low = (r // pc) % pc, r % pc
        if d == 1:
            return high
        if d == 3:
            return low
        return jnp.where(self.face(r) // 2 == 0, high, low)

    def fine_fine(self, small, d):
        return expand(small, self.n, self.fine(d), self.n, self.fine(d))

    def kron(self, time, x, y, z):
        return self.fine_fine(time, 0) * self.fine_fine(x, 1) * self.fine_fine(y, 2) * self.fine_fine(z, 3)

    def restricted(self, time, x, y, z):
        total = expand(time, self.nc, lambda r: r * 0, self.n, self.fine(0))
        for d, small in ((1, x), (2, y), (3, z)):
            total = total * expand(small, self.nc, self.coarse(d), self.n, self.fine(d))
        return total

    def prolonged(self, time_t, space_t):
        total = expand(time_t, self.n, self.fine(0), self.nc, lambda r: r * 0)
        for d in (1, 2, 3):
            total = total * expand(space_t, self.n, self.fine(d), self.nc, self.coarse(d))
        return total

    def coarse_coarse(self, small):
        total = 1.0
        for d in (1, 2, 3):
            total = total * expand(small, self.nc, self.coarse(d), self.nc, self.coarse(d))
        return total

    def face_traces(self, time, space):
        shape = (self.nf, self.n)
        row, col = iota(shape, 0), iota(shape, 1)
        face = self.face(row)
        opposite = jnp.where(face % 2 == 0, self.p - 1, 0)
        total = expand(time, self.nf, lambda r: r * 0, self.n, self.fine(0))
        for d in (1, 2, 3):
            tangential = expand(space, self.nf, functools.partial(self.bit, d), self.n, self.fine(d))
            normal = (self.fine(d)(col) == opposite).astype(F32)
            total = total * jnp.where(face // 2 == d - 1, normal, tangential)
        return total

    def face_spread(self, space):
        shape = (self.nc, self.nf)
        row, col = iota(shape, 0), iota(shape, 1)
        face = self.face(col)
        total = 1.0
        node = lambda r: jnp.where(self.face(r) % 2 == 0, 0, self.p - 1)
        for d in (1, 2, 3):
            normal = expand(space, self.nc, self.coarse(d), self.nf, node)
            tangential = (self.coarse(d)(row) == self.bit(d, col)).astype(F32)
            total = total * jnp.where(face // 2 == d - 1, normal, tangential)
        return total


def two_minus(small):
    n = small.shape[0]
    return 2.0 * (iota((n, n), 0) == iota((n, n), 1)).astype(F32) - small


def pieces(v):
    high = v.astype(BF16)
    return high, (v - high.astype(F32)).astype(BF16)


def bdot(a, b):
    return jnp.dot(a, b, preferred_element_type=F32)


def product(matrix, values):
    mh, ml = matrix
    vh, vl = values
    return bdot(mh, vh) + (bdot(mh, vl) + bdot(ml, vh))


def select_columns(values, indices, count):
    rows = values.shape[0]
    high, low = pieces(values)
    chosen = (iota((count, indices.shape[-1]), 0) == indices).astype(F32).astype(BF16)
    both = bdot(jnp.concatenate([high, low], axis=0), chosen)
    return both[:rows] + both[rows:]


def lower_half(shape):
    return iota(shape, 0) < 4


def trace_rows(ref, rows, face, p):
    d, node = face // 2, face % 2 * (p - 1)
    if d == 0:
        step = p * p
        return jnp.concatenate(
            [ref[r + node * step : r + (node + 1) * step, :] for r in range(0, rows, p * step)], axis=0
        )
    if d == 1:
        parts = []
        at = node * p // 8 * 8
        for r in range(0, rows, 2 * p * p):
            first = ref[r + at : r + at + 8, :]
            second = ref[r + p * p + at : r + p * p + at + 8, :]
            low = lower_half(first.shape)
            if node == 0:
                parts.append(jnp.where(low, first, pltpu.roll(second, 4, 0)))
            else:
                parts.append(jnp.where(low, pltpu.roll(first, 4, 0), second))
        return jnp.concatenate(parts, axis=0)
    raise ValueError(face)


def to_tiles(tiles_ref, ref):
    for k in range(tiles_ref.shape[0]):
        tiles_ref[k] = ref[:, 128 * k : 128 * k + 128]


def z_trace_rows(tiles_ref, rows, face, p):
    node = face % 2 * (p - 1)
    parts = [tiles_ref[k, pl.ds(node, rows // p, stride=p), :] for k in range(tiles_ref.shape[0])]
    return jnp.concatenate(parts, axis=1)


def z_put_rows(tiles_ref, values, rows, face, p):
    node = face % 2 * (p - 1)
    for k in range(tiles_ref.shape[0]):
        tiles_ref[k, pl.ds(node, rows // p, stride=p), :] = values[:, 128 * k : 128 * k + 128]


def add_rows(ref, values, rows, face, p):
    d, node = face // 2, face % 2 * (p - 1)
    if d == 0:
        step = p * p
        for i, r in enumerate(range(0, rows, p * step)):
            at = r + node * step
            ref[at : at + step, :] += values[i * step : (i + 1) * step]
    elif d == 1:
        at = node * p // 8 * 8
        for i, r in enumerate(range(0, rows, 2 * p * p)):
            eight = values[8 * i : 8 * i + 8]
            turned = pltpu.roll(eight, 4, 0)
            low = lower_half(eight.shape)
            if node == 0:
                first, second = jnp.where(low, eight, 0.0), jnp.where(low, turned, 0.0)
            else:
                first, second = jnp.where(low, 0.0, turned), jnp.where(low, 0.0, eight)
            ref[r + at : r + at + 8, :] += first
            ref[r + p * p + at : r + p * p + at + 8, :] += second


def last_time(nodes):
    return (nodes.q - 1) * nodes.p**3


def pack(x_ref, halo_ref, parity_ref, first_ref, second_ref, rows, p):
    elements = x_ref.shape[-1]
    to_left = select_columns(trace_rows(x_ref, rows, 0, p), halo_ref[0:1, :], elements)
    to_right = select_columns(trace_rows(x_ref, rows, 1, p), halo_ref[1:2, :], elements)
    even = parity_ref[0] == 0
    first_ref[...] = jnp.where(even, to_right, to_left)
    second_ref[...] = jnp.where(even, to_left, to_right)


def start_kernel(nodes, parity, f_ref, c_ref, halo_ref, tb, sb, tr, sr, x_ref, first_ref, second_ref, last_ref, rf_ref):
    n, p = nodes.n, nodes.p
    rows = f_ref.shape[0]
    ti, si = two_minus(tb[...]), two_minus(sb[...])
    inverse = pieces(nodes.kron(ti, si, si, si))
    scale = 1.0 / c_ref[...]
    total = 0.0
    for s in range(rows // n):
        f = f_ref[s * n : (s + 1) * n, :]
        total = total + f
        x_ref[s * n : (s + 1) * n, :] = product(inverse, pieces(f)) * scale
    pack(x_ref, halo_ref, parity, first_ref, second_ref, rows, p)
    at = rows - n + last_time(nodes)
    last_ref[...] = x_ref[at:rows, :]
    rf_ref[...] = product(pieces(nodes.restricted(tr[...], sr[...], sr[...], sr[...])), pieces(total))


def local_kernel(nodes, x_ref, x1_ref, c_ref, nb_ref, tb, sb, st, out_ref, g_ref, tiles_ref):
    n, p = nodes.n, nodes.p
    rows, elements = x_ref.shape
    plane = p**3
    ti, si = two_minus(tb[...]), two_minus(sb[...])
    tit, sis, sid = exact(ti, tb[...]), exact(si, sb[...]), exact(si, st[...])
    et = nodes.fine_fine(ti, 0)
    es = [nodes.fine_fine(si, d) for d in (1, 2, 3)]
    ed = [nodes.fine_fine(sid, d) for d in (1, 2, 3)]
    inverse = pieces(et * es[0] * es[1] * es[2])
    unit = (iota((n, n), 0) == iota((n, n), 1)).astype(F32)
    keep = pieces(unit - nodes.kron(tit, sis, sis, sis))
    drift = pieces(-et * (ed[0] * es[1] * es[2] + es[0] * ed[1] * es[2] + es[0] * es[1] * ed[2]))
    c = c_ref[...]
    scale = 1.0 / c
    g_ref[...] = jnp.zeros_like(g_ref)
    for s in range(1, rows // n):
        before = (s - 1) * n + last_time(nodes)
        g_ref[s * n : s * n + plane, :] = UPWIND * c * x_ref[before : before + plane, :]
    to_tiles(tiles_ref, x_ref)
    z_values = [z_trace_rows(tiles_ref, rows, face ^ 1, p) for face in (4, 5)]
    tiles_ref[...] = jnp.zeros_like(tiles_ref)
    for face in range(6):
        values = trace_rows(x_ref, rows, face ^ 1, p) if face < 4 else z_values[face - 4]
        coupled = PENALTY * select_columns(values, nb_ref[face : face + 1, :], elements)
        if face < 4:
            add_rows(g_ref, coupled, rows, face, p)
        else:
            z_put_rows(tiles_ref, coupled, rows, face, p)
    for k in range(tiles_ref.shape[0]):
        g_ref[:, 128 * k : 128 * k + 128] += tiles_ref[k]
    for s in range(rows // n):
        here = slice(s * n, (s + 1) * n)
        x = pieces(x_ref[here, :])
        turned = product(drift, x) + product(inverse, pieces(g_ref[here, :]))
        out_ref[here, :] = x1_ref[here, :] + product(keep, x) + scale * turned


def ghosts(parity_ref, got_first_ref, got_second_ref):
    even = parity_ref[0] == 0
    first, second = got_first_ref[...], got_second_ref[...]
    return jnp.where(even, second, first), jnp.where(even, first, second)


def finish(nodes, parity, base_ref, got_first, got_second, prev_a, prev_b, c_ref, nb_ref, tb, sb, x_ref, g_ref):
    n, p = nodes.n, nodes.p
    rows, elements = base_ref.shape
    ti, si = two_minus(tb[...]), two_minus(sb[...])
    inverse = pieces(nodes.kron(ti, si, si, si))
    c = c_ref[...]
    scale = 1.0 / c
    left, right = ghosts(parity, got_first, got_second)
    count = left.shape[-1]
    g_ref[...] = jnp.zeros_like(g_ref)
    g_ref[: p**3, :] = UPWIND * c * (prev_a[...] + prev_b[...])
    add_rows(g_ref, PENALTY * select_columns(left, nb_ref[0:1, :] - elements, count), rows, 0, p)
    add_rows(g_ref, PENALTY * select_columns(right, nb_ref[1:2, :] - (elements + count), count), rows, 1, p)
    for s in range(rows // n):
        here = slice(s * n, (s + 1) * n)
        x_ref[here, :] = base_ref[here, :] + scale * product(inverse, pieces(g_ref[here, :]))


def finish_kernel(
    nodes, parity, base_ref, got_first, got_second, prev_a, prev_b, c_ref, nb_ref, halo_ref, tb, sb,
    x_ref, first_ref, second_ref, last_ref, g_ref,
):
    finish(nodes, parity, base_ref, got_first, got_second, prev_a, prev_b, c_ref, nb_ref, tb, sb, x_ref, g_ref)
    rows = base_ref.shape[0]
    pack(x_ref, halo_ref, parity, first_ref, second_ref, rows, nodes.p)
    last_ref[...] = x_ref[rows - nodes.n + last_time(nodes) : rows, :]


def coarse_kernel(
    nodes, parity, base_ref, got_first, got_second, prev_a, prev_b, c_ref, nb_ref, halo_ref, rf_ref, tb, sb, st, tr, sr,
    x_ref, first_ref, second_ref, local_ref, g_ref,
):
    finish(nodes, parity, base_ref, got_first, got_second, prev_a, prev_b, c_ref, nb_ref, tb, sb, x_ref, g_ref)
    n, p, nc = nodes.n, nodes.p, nodes.nc
    rows, elements = x_ref.shape
    t, s = tr[...], sr[...]
    tk, sk, sd = exact(t, tb[...]), exact(s, sb[...]), exact(s, st[...])
    block = nodes.restricted(tk, sk, sk, sk)
    stiff = nodes.restricted(t, sd, s, s) + nodes.restricted(t, s, sd, s) + nodes.restricted(t, s, s, sd)
    faces = nodes.face_traces(t, s)
    stacked = pieces(jnp.concatenate([block, stiff, faces], axis=0))
    total = x_ref[:n, :]
    before = 0.0
    for k in range(1, rows // n):
        total = total + x_ref[k * n : (k + 1) * n, :]
        at = (k - 1) * n + last_time(nodes)
        before = before + x_ref[at : at + p**3, :]
    applied = product(stacked, pieces(total))
    first_node = pieces(nodes.restricted(t, s, s, s)[:, : p**3])
    c = c_ref[...]
    local = rf_ref[...] - c * applied[:nc] - applied[nc : 2 * nc]
    local = local + (UPWIND * c) * product(first_node, pieces(before))
    traces = applied[2 * nc :]
    high, low = pieces(traces)
    both = jnp.concatenate([high, low], axis=0)
    four = nodes.pc**2
    row = iota((nodes.nf, elements), 0) // four
    coupled = 0.0
    for face in range(6):
        chosen = (iota((elements, elements), 0) == nb_ref[face : face + 1, :]).astype(F32).astype(BF16)
        got = bdot(both, chosen)
        coupled = coupled + jnp.where(row == face, got[: nodes.nf] + got[nodes.nf :], 0.0)
    spread = nodes.face_spread(s)
    local_ref[:nc, :] = local + PENALTY * exact(spread, coupled)
    end = x_ref[rows - n + last_time(nodes) : rows, :]
    local_ref[nc:, :] = UPWIND * product(first_node, pieces(end))
    to_left = select_columns(traces[:8], halo_ref[0:1, :], elements)
    to_right = select_columns(traces[:8], halo_ref[1:2, :], elements)
    even = parity[0] == 0
    first_ref[...] = jnp.where(even, to_right, to_left)
    second_ref[...] = jnp.where(even, to_left, to_right)


def group_kernel(nodes, parity, local_ref, got_first, got_second, c_ref, nb_ref, sr, cs, out_ref):
    nc = nodes.nc
    elements = local_ref.shape[-1]
    left, right = ghosts(parity, got_first, got_second)
    count = left.shape[-1]
    from_left = select_columns(left, nb_ref[0:1, :] - elements, count)
    from_right = select_columns(right, nb_ref[1:2, :] - (elements + count), count)
    low = iota((8, elements), 0) < nodes.pc**2
    both = jnp.where(low, from_left, from_right)
    spread = nodes.face_spread(sr[...])[:, :8]
    scale = 1.0 / c_ref[...]
    total = (local_ref[:nc, :] + PENALTY * exact(spread, both)) * scale
    smoother = nodes.coarse_coarse(cs[...])
    out_ref[:nc, :] = exact(smoother, total)
    out_ref[nc:, :] = exact(smoother, local_ref[nc:, :])


def end_kernel(nodes, group, every_ref, x_ref, cs, trt, srt, out_ref):
    nc, n = nodes.nc, nodes.n
    transfer = COARSE_UPWIND * nodes.coarse_coarse(cs[...])
    mine = group[0]
    peers = every_ref.shape[0] // (2 * nc)
    state = jnp.zeros((nc, x_ref.shape[-1]), F32)
    for g in range(peers):
        at = 2 * nc * g
        after = exact(transfer, state) + every_ref[at : at + nc, :]
        if g:
            after = after + every_ref[at - nc : at, :]
        state = jnp.where(g <= mine, after, state)
    lifted = product(pieces(nodes.prolonged(trt[...], srt[...])), pieces(state))
    for s in range(x_ref.shape[0] // n):
        here = slice(s * n, (s + 1) * n)
        out_ref[here, :] = x_ref[here, :] + lifted


def call(kernel, nodes, outs, scratch=(), scalars=1):
    smem = [pl.BlockSpec(memory_space=pltpu.SMEM)] * scalars

    def run(*args):
        in_specs = smem + [pl.BlockSpec(memory_space=pltpu.VMEM)] * (len(args) - scalars)
        return pl.pallas_call(
            functools.partial(kernel, nodes),
            out_shape=[jax.ShapeDtypeStruct(shape, F32) for shape in outs],
            in_specs=in_specs,
            out_specs=[pl.BlockSpec(memory_space=pltpu.VMEM)] * len(outs),
            scratch_shapes=[pltpu.VMEM(shape, F32) for shape in scratch],
            compiler_params=pltpu.CompilerParams(vmem_limit_bytes=VMEM_BYTES),
            name=kernel.__name__,
        )(*args)

    return run


def swapped(first, second):
    peers = lax.axis_size("space")
    pairs = [[], []]
    for i in range(peers - 1):
        pairs[i % 2] += [(i, i + 1), (i + 1, i)]
    return [lax.ppermute(v, "space", q) for v, q in zip((first, second), pairs)]


def handed_on(last):
    peers = lax.axis_size("slab")
    return [lax.ppermute(last, "slab", [(i, i + 1) for i in range(k, peers - 1, 2)]) for k in (0, 1)]


def body(
    forcing, coefficient, neighbours, halo_faces, time_block, space_block, stiffness, time_restrict, space_restrict,
    coarse_smoother,
):
    slabs, q, p = forcing.shape[:3]
    elements = forcing.shape[-1]
    nodes = Nodes(q, p, space_restrict.shape[0])
    rows = slabs * nodes.n
    count = halo_faces.shape[-1]
    f = forcing.reshape(rows, elements)
    c = coefficient.reshape(1, elements)
    parity = (lax.axis_index("space") % 2).astype(jnp.int32).reshape(1)
    group = lax.axis_index("slab").astype(jnp.int32).reshape(1)
    field = (rows, elements)
    face = (rows // p, count)
    plane = (p**3, elements)
    nc = nodes.nc
    x1, first, second, last, rf = call(start_kernel, nodes, (field, face, face, plane, (nc, elements)))(
        parity, f, c, halo_faces, time_block, space_block, time_restrict, space_restrict
    )
    x = x1
    for sweep in range(SWEEPS - 1):
        got = swapped(first, second) + handed_on(last)
        (base,) = call(local_kernel, nodes, (field,), (field, (elements // 128, rows, 128)), 0)(
            x, x1, c, neighbours, time_block, space_block, stiffness
        )
        if sweep < SWEEPS - 2:
            x, first, second, last = call(finish_kernel, nodes, (field, face, face, plane), (field,))(
                parity, base, *got, c, neighbours, halo_faces, time_block, space_block
            )
        else:
            x, first, second, local = call(
                coarse_kernel, nodes, (field, (8, count), (8, count), (2 * nc, elements)), (field,)
            )(
                parity, base, *got, c, neighbours, halo_faces, rf, time_block, space_block, stiffness,
                time_restrict, space_restrict,
            )
    got = swapped(first, second)
    (mine,) = call(group_kernel, nodes, ((2 * nc, elements),))(
        parity, local, *got, c, neighbours, space_restrict, coarse_smoother
    )
    every = lax.all_gather(mine, "slab", axis=0, tiled=True)
    (out,) = call(end_kernel, nodes, (field,))(
        group, every, x, coarse_smoother, time_restrict.T, space_restrict.T
    )
    return out.reshape(forcing.shape)


def solution(mesh):
    in_specs = (
        P("slab", None, None, None, None, "space"),
        P("space"),
        P(None, "space"),
        P(None, "space"),
        P(),
        P(),
        P(),
        P(),
        P(),
        P(),
    )
    out_specs = P("slab", None, None, None, None, "space")
    return jax.shard_map(body, mesh=mesh, in_specs=in_specs, out_specs=out_specs, check_vma=False)
```

profile of v0, /device:TPU:9, one launch (start us, length us, event | category | flops | bytes accessed | tf_op | source)
XLA Modules:
  0.0 93.6 jit_solution(5232875967192694415)
XLA Ops:
  0.0 2.7 %reshape.17.f_ref = f32[384,1024]{1,0:T(8,128)} reshape(f32[2,3,4,4,4,1024]{5,4,3,2,1,0:T(4,128)} %param.10) | data formatting | bytes 3145728 | tf_op jit(solution)/shard_map/reshape | solution.py:426
  2.7 5.5 %start_kernel.1 = (f32[384,1024]{1,0:T(8,128)}, f32[96,512]{1,0:T(8,128)}, f32[96,512]{1,0:T(8,128)}, f32[64,1024]{1,0:T(8,128)}, f32[8,1024]{1,0:T(8,128)}) custom-call(s32[1]{0:T(128)} %bitcast.1.parity, f32[384,1024]{1,0:T(8,128)} %reshape.17.f_ref, f32[1,1024]{1,0:T(1,128)} %bitcast.5, s32[2,512]{1,0:T(2,128)} %halo_ref.5, f32[3,3]{1,0:T(4,128)} %tb.9, ...), custom_call_target="tpu_custom_call" | custom-call | tf_op jit(solution)/shard_map/start_kernel/pallas_call | solution.py:391
  8.2 1.3 %collective-permute-start.2 = (f32[64,1024]{1,0:T(8,128)}, f32[64,1024]{1,0:T(8,128)S(1)}, u32[]{:S(2)}, u32[]{:S(2)}) collective-permute-start(f32[64,1024]{1,0:T(8,128)} %get-tuple-element.21), channel_id=1, source_target_pairs={{0,8},{16,24},{1,9},{17,25},{2,10},{18,26},{3,11},{19,27},{4,12},{... | collective-permute-start | bytes 786440 | tf_op jit(solution)/shard_map/ppermute | solution.py:414
  9.5 4.2 %collective-permute-start.3 = (f32[64,1024]{1,0:T(8,128)}, f32[64,1024]{1,0:T(8,128)S(1)}, u32[]{:S(2)}, u32[]{:S(2)}) collective-permute-start(f32[64,1024]{1,0:T(8,128)} %get-tuple-element.21), channel_id=1, source_target_pairs={{8,16},{9,17},{10,18},{11,19},{12,20},{13,21},{14,22},{15,23}} | collective-permute-start | bytes 786440 | tf_op jit(solution)/shard_map/ppermute | solution.py:414
  13.7 1.3 %collective-permute-start = (f32[96,512]{1,0:T(8,128)}, f32[96,512]{1,0:T(8,128)S(1)}, u32[]{:S(2)}, u32[]{:S(2)}) collective-permute-start(f32[96,512]{1,0:T(8,128)} %get-tuple-element.19), channel_id=1, source_target_pairs={{0,1},{1,0},{2,3},{3,2},{4,5},{5,4},{6,7},{7,6},{8,9},{9,8},{10,11... | collective-permute-start | bytes 589832 | tf_op jit(solution)/shard_map/ppermute | solution.py:409
  15.0 2.2 %collective-permute-start.1 = (f32[96,512]{1,0:T(8,128)}, f32[96,512]{1,0:T(8,128)S(1)}, u32[]{:S(2)}, u32[]{:S(2)}) collective-permute-start(f32[96,512]{1,0:T(8,128)} %get-tuple-element.20), channel_id=1, source_target_pairs={{1,2},{2,1},{3,4},{4,3},{5,6},{6,5},{9,10},{10,9},{11,12},{12,11},... | collective-permute-start | bytes 589832 | tf_op jit(solution)/shard_map/ppermute | solution.py:409
  17.2 11.6 %local_kernel.2.base_ref = f32[384,1024]{1,0:T(8,128)} custom-call(f32[384,1024]{1,0:T(8,128)} %get-tuple-element.18.x_ref.x1_ref, f32[384,1024]{1,0:T(8,128)} %get-tuple-element.18.x_ref.x1_ref, f32[1,1024]{1,0:T(1,128)} %bitcast.6, s32[6,1024]{1,0:T(8,128)} %nb_ref.9, f32[3,3]{1,0:T(4,128)} %tb.9, f32[4,4]{1,0:T(4,128)} %sb.9, f32[4,4]{1,0:T(4,128)} %st.5), custom_call_target="tpu_custom_call" | custom-call | tf_op jit(solution)/shard_map/local_kernel/pallas_call | solution.py:391
  29.6 0.7 copy-done.3
  30.3 5.9 %finish_kernel.1 = (f32[384,1024]{1,0:T(8,128)}, f32[96,512]{1,0:T(8,128)}, f32[96,512]{1,0:T(8,128)}, f32[64,1024]{1,0:T(8,128)}) custom-call(s32[1]{0:T(128)} %bitcast.1.parity, f32[384,1024]{1,0:T(8,128)} %local_kernel.2.base_ref, f32[96,512]{1,0:T(8,128)} %copy-done.6, f32[96,512]{1,0:T(8,128)} %copy-done.7, f32[64,1024]{1,0:T(8,128)} %copy-done.2, ...), custom_call_target="tpu_custom_call" | custom-call | tf_op jit(solution)/shard_map/finish_kernel/pallas_call | solution.py:391
  36.2 1.3 %collective-permute-start.6 = (f32[64,1024]{1,0:T(8,128)}, f32[64,1024]{1,0:T(8,128)S(1)}, u32[]{:S(2)}, u32[]{:S(2)}) collective-permute-start(f32[64,1024]{1,0:T(8,128)} %get-tuple-element.25), channel_id=1, source_target_pairs={{0,8},{16,24},{1,9},{17,25},{2,10},{18,26},{3,11},{19,27},{4,12},{... | collective-permute-start | bytes 786440 | tf_op jit(solution)/shard_map/ppermute | solution.py:414
  37.5 1.9 %collective-permute-start.7 = (f32[64,1024]{1,0:T(8,128)}, f32[64,1024]{1,0:T(8,128)S(1)}, u32[]{:S(2)}, u32[]{:S(2)}) collective-permute-start(f32[64,1024]{1,0:T(8,128)} %get-tuple-element.25), channel_id=1, source_target_pairs={{8,16},{9,17},{10,18},{11,19},{12,20},{13,21},{14,22},{15,23}} | collective-permute-start | bytes 786440 | tf_op jit(solution)/shard_map/ppermute | solution.py:414
  39.3 2.4 %collective-permute-start.4 = (f32[96,512]{1,0:T(8,128)}, f32[96,512]{1,0:T(8,128)S(1)}, u32[]{:S(2)}, u32[]{:S(2)}) collective-permute-start(f32[96,512]{1,0:T(8,128)} %get-tuple-element.23), channel_id=1, source_target_pairs={{0,1},{1,0},{2,3},{3,2},{4,5},{5,4},{6,7},{7,6},{8,9},{9,8},{10,11... | collective-permute-start | bytes 589832 | tf_op jit(solution)/shard_map/ppermute | solution.py:409
  41.8 2.1 %collective-permute-start.5 = (f32[96,512]{1,0:T(8,128)}, f32[96,512]{1,0:T(8,128)S(1)}, u32[]{:S(2)}, u32[]{:S(2)}) collective-permute-start(f32[96,512]{1,0:T(8,128)} %get-tuple-element.24), channel_id=1, source_target_pairs={{1,2},{2,1},{3,4},{4,3},{5,6},{6,5},{9,10},{10,9},{11,12},{12,11},... | collective-permute-start | bytes 589832 | tf_op jit(solution)/shard_map/ppermute | solution.py:409
  43.9 11.5 %local_kernel.3.base_ref = f32[384,1024]{1,0:T(8,128)} custom-call(f32[384,1024]{1,0:T(8,128)} %get-tuple-element.22.x_ref, f32[384,1024]{1,0:T(8,128)} %get-tuple-element.18.x_ref.x1_ref, f32[1,1024]{1,0:T(1,128)} %bitcast.8, s32[6,1024]{1,0:T(8,128)} %nb_ref.9, f32[3,3]{1,0:T(4,128)} %tb.9, f32[4,4]{1,0:T(4,128)} %sb.9, f32[4,4]{1,0:T(4,128)} %st.5), custom_call_target="tpu_custom_call" | custom-call | tf_op jit(solution)/shard_map/local_kernel/pallas_call | solution.py:391
  56.4 10.2 %coarse_kernel.1 = (f32[384,1024]{1,0:T(8,128)}, f32[8,512]{1,0:T(8,128)}, f32[8,512]{1,0:T(8,128)}, f32[16,1024]{1,0:T(8,128)}) custom-call(s32[1]{0:T(128)} %bitcast.1.parity, f32[384,1024]{1,0:T(8,128)} %local_kernel.3.base_ref, f32[96,512]{1,0:T(8,128)} %copy-done.4, f32[96,512]{1,0:T(8,128)} %copy-done.5, f32[64,1024]{1,0:T(8,128)} %copy-done, ...), custom_call_target="tpu_custom_call" | custom-call | tf_op jit(solution)/shard_map/coarse_kernel/pallas_call | solution.py:391
  66.5 2.5 %collective-permute-start.8 = (f32[8,512]{1,0:T(8,128)}, f32[8,512]{1,0:T(8,128)S(1)}, u32[]{:S(2)}, u32[]{:S(2)}) collective-permute-start(f32[8,512]{1,0:T(8,128)} %get-tuple-element.28), channel_id=1, source_target_pairs={{0,1},{1,0},{2,3},{3,2},{4,5},{5,4},{6,7},{7,6},{8,9},{9,8},{10,11... | collective-permute-start | bytes 49160 | tf_op jit(solution)/shard_map/ppermute | solution.py:409
  69.0 1.9 %collective-permute-start.9 = (f32[8,512]{1,0:T(8,128)}, f32[8,512]{1,0:T(8,128)S(1)}, u32[]{:S(2)}, u32[]{:S(2)}) collective-permute-start(f32[8,512]{1,0:T(8,128)} %get-tuple-element.29), channel_id=1, source_target_pairs={{1,2},{2,1},{3,4},{4,3},{5,6},{6,5},{9,10},{10,9},{11,12},{12,11},... | collective-permute-start | bytes 49160 | tf_op jit(solution)/shard_map/ppermute | solution.py:409
  70.9 0.7 copy.11
  71.6 0.7 copy.12.trt
  72.3 2.3 %collective-permute-done.9.got_second = f32[8,512]{1,0:T(8,128)S(1)} collective-permute-done((f32[8,512]{1,0:T(8,128)}, f32[8,512]{1,0:T(8,128)S(1)}, u32[]{:S(2)}, u32[]{:S(2)}) %collective-permute-start.9) | collective-permute-done | bytes 16416 | tf_op jit(solution)/shard_map/ppermute | solution.py:409
  75.2 2.7 %group_kernel.1 = f32[16,1024]{1,0:T(8,128)} custom-call(s32[1]{0:T(128)} %bitcast.1.parity, f32[16,1024]{1,0:T(8,128)} %get-tuple-element.27.local_ref, f32[8,512]{1,0:T(8,128)} %copy-done.9, f32[8,512]{1,0:T(8,128)} %copy-done.10, f32[1,1024]{1,0:T(1,128)} %bitcast.10, s32[6,1024]{1,0:T(8,128)} %nb_ref.9, f32[2,4]{1,0:T(2,128)} %sr.5, f32[2,2]{1,0:T(2,128)} %cs.3), custom_call_target="tpu_custom_call" | custom-call | tf_op jit(solution)/shard_map/group_kernel/pallas_call | solution.py:391
  77.9 8.2 %all_gather.3.every_ref = f32[64,1024]{1,0:T(8,128)} all-gather(f32[16,1024]{1,0:T(8,128)} %group_kernel.1), channel_id=1, replica_groups=mesh['slab'=4,'space'=8] {'slab'}, dimensions={0}, use_global_device_ids=true | all-gather | bytes 327680 | tf_op jit(solution)/shard_map/all_gather | solution.py:458
  86.1 4.8 %end_kernel.1 = f32[384,1024]{1,0:T(8,128)} custom-call(s32[1]{0:T(128)} %bitcast.group, f32[64,1024]{1,0:T(8,128)} %all_gather.3.every_ref, f32[384,1024]{1,0:T(8,128)} %get-tuple-element.30.x_ref, f32[2,2]{1,0:T(2,128)} %cs.3, f32[3,1]{1,0:T(4,128)} %copy.12.trt, f32[4,2]{1,0:T(4,128)} %bitcast.11), custom_call_target="tpu_custom_call" | custom-call | tf_op jit(solution)/shard_map/end_kernel/pallas_call | solution.py:391
  90.9 2.7 %reshape.19 = f32[2,3,4,4,4,1024]{5,4,3,2,1,0:T(4,128)} reshape(f32[384,1024]{1,0:T(8,128)} %end_kernel.1) | data formatting | bytes 3145728 | tf_op jit(solution)/shard_map/reshape | solution.py:462
  (32 shorter events, 2.3 us)
Async XLA Ops:
  8.2 20.5 %collective-permute-start.2 = (f32[64,1024]{1,0:T(8,128)}, f32[64,1024]{1,0:T(8,128)S(1)}, u32[]{:S(2)}, u32[]{:S(2)}) collective-permute-start(f32[64,1024]{1,0:T(8,128)} %get-tuple-element.21), channel_id=1, source_target_pairs={{0,8},{16,24},{1,9},{17,25},{2,10},{18,26},{3,11},{19,27},{4,12},{... | collective-permute-start | bytes 786440 | tf_op jit(solution)/shard_map/ppermute | solution.py:414
  9.5 19.3 %collective-permute-start.3 = (f32[64,1024]{1,0:T(8,128)}, f32[64,1024]{1,0:T(8,128)S(1)}, u32[]{:S(2)}, u32[]{:S(2)}) collective-permute-start(f32[64,1024]{1,0:T(8,128)} %get-tuple-element.21), channel_id=1, source_target_pairs={{8,16},{9,17},{10,18},{11,19},{12,20},{13,21},{14,22},{15,23}} | collective-permute-start | bytes 786440 | tf_op jit(solution)/shard_map/ppermute | solution.py:414
  13.7 15.1 %collective-permute-start = (f32[96,512]{1,0:T(8,128)}, f32[96,512]{1,0:T(8,128)S(1)}, u32[]{:S(2)}, u32[]{:S(2)}) collective-permute-start(f32[96,512]{1,0:T(8,128)} %get-tuple-element.19), channel_id=1, source_target_pairs={{0,1},{1,0},{2,3},{3,2},{4,5},{5,4},{6,7},{7,6},{8,9},{9,8},{10,11... | collective-permute-start | bytes 589832 | tf_op jit(solution)/shard_map/ppermute | solution.py:409
  15.0 13.8 %collective-permute-start.1 = (f32[96,512]{1,0:T(8,128)}, f32[96,512]{1,0:T(8,128)S(1)}, u32[]{:S(2)}, u32[]{:S(2)}) collective-permute-start(f32[96,512]{1,0:T(8,128)} %get-tuple-element.20), channel_id=1, source_target_pairs={{1,2},{2,1},{3,4},{4,3},{5,6},{6,5},{9,10},{10,9},{11,12},{12,11},... | collective-permute-start | bytes 589832 | tf_op jit(solution)/shard_map/ppermute | solution.py:409
  28.7 0.7 copy-start.6
  28.7 0.7 copy-start.7
  28.7 0.8 copy-start.2
  29.6 0.7 copy-start.3
  36.2 19.3 %collective-permute-start.6 = (f32[64,1024]{1,0:T(8,128)}, f32[64,1024]{1,0:T(8,128)S(1)}, u32[]{:S(2)}, u32[]{:S(2)}) collective-permute-start(f32[64,1024]{1,0:T(8,128)} %get-tuple-element.25), channel_id=1, source_target_pairs={{0,8},{16,24},{1,9},{17,25},{2,10},{18,26},{3,11},{19,27},{4,12},{... | collective-permute-start | bytes 786440 | tf_op jit(solution)/shard_map/ppermute | solution.py:414
  37.5 18.0 %collective-permute-start.7 = (f32[64,1024]{1,0:T(8,128)}, f32[64,1024]{1,0:T(8,128)S(1)}, u32[]{:S(2)}, u32[]{:S(2)}) collective-permute-start(f32[64,1024]{1,0:T(8,128)} %get-tuple-element.25), channel_id=1, source_target_pairs={{8,16},{9,17},{10,18},{11,19},{12,20},{13,21},{14,22},{15,23}} | collective-permute-start | bytes 786440 | tf_op jit(solution)/shard_map/ppermute | solution.py:414
  39.3 16.1 %collective-permute-start.4 = (f32[96,512]{1,0:T(8,128)}, f32[96,512]{1,0:T(8,128)S(1)}, u32[]{:S(2)}, u32[]{:S(2)}) collective-permute-start(f32[96,512]{1,0:T(8,128)} %get-tuple-element.23), channel_id=1, source_target_pairs={{0,1},{1,0},{2,3},{3,2},{4,5},{5,4},{6,7},{7,6},{8,9},{9,8},{10,11... | collective-permute-start | bytes 589832 | tf_op jit(solution)/shard_map/ppermute | solution.py:409
  41.8 13.7 %collective-permute-start.5 = (f32[96,512]{1,0:T(8,128)}, f32[96,512]{1,0:T(8,128)S(1)}, u32[]{:S(2)}, u32[]{:S(2)}) collective-permute-start(f32[96,512]{1,0:T(8,128)} %get-tuple-element.24), channel_id=1, source_target_pairs={{1,2},{2,1},{3,4},{4,3},{5,6},{6,5},{9,10},{10,9},{11,12},{12,11},... | collective-permute-start | bytes 589832 | tf_op jit(solution)/shard_map/ppermute | solution.py:409
  55.4 15.5 %copy-start.8 = (f32[2,4]{1,0:T(2,128)S(1)}, f32[2,4]{1,0:T(2,128)}, u32[]{:S(2)}) copy-start(f32[2,4]{1,0:T(2,128)} %sr.5) | copy-start | bytes 100
  55.4 16.2 %copy-start.11 = (f32[1,3]{1,0:T(1,128)S(1)}, f32[1,3]{1,0:T(1,128)}, u32[]{:S(2)}) copy-start(f32[1,3]{1,0:T(1,128)} %tr.3) | copy-start | bytes 40
  55.4 0.7 copy-start.4
  55.4 0.7 copy-start.5
  55.5 0.8 copy-start
  55.5 0.9 copy-start.1
  66.5 5.8 %collective-permute-start.8 = (f32[8,512]{1,0:T(8,128)}, f32[8,512]{1,0:T(8,128)S(1)}, u32[]{:S(2)}, u32[]{:S(2)}) collective-permute-start(f32[8,512]{1,0:T(8,128)} %get-tuple-element.28), channel_id=1, source_target_pairs={{0,1},{1,0},{2,3},{3,2},{4,5},{5,4},{6,7},{7,6},{8,9},{9,8},{10,11... | collective-permute-start | bytes 49160 | tf_op jit(solution)/shard_map/ppermute | solution.py:409
  69.0 5.6 %collective-permute-start.9 = (f32[8,512]{1,0:T(8,128)}, f32[8,512]{1,0:T(8,128)S(1)}, u32[]{:S(2)}, u32[]{:S(2)}) collective-permute-start(f32[8,512]{1,0:T(8,128)} %get-tuple-element.29), channel_id=1, source_target_pairs={{1,2},{2,1},{3,4},{4,3},{5,6},{6,5},{9,10},{10,9},{11,12},{12,11},... | collective-permute-start | bytes 49160 | tf_op jit(solution)/shard_map/ppermute | solution.py:409
  72.3 2.3 %copy-start.9 = (f32[8,512]{1,0:T(8,128)}, f32[8,512]{1,0:T(8,128)S(1)}, u32[]{:S(2)}) copy-start(f32[8,512]{1,0:T(8,128)S(1)} %collective-permute-done.8.got_first) | copy-start | bytes 49156
  74.6 0.6 copy-start.10
where the time goes:
time: 94.1 us; the launch traced here: 93.6 us
  Pallas kernels  52.1 us (55%)
  starting transfers between devices  21 us (22%)
  local copies, waits for them, and re-layouts  9.79 us (10%)
  blocking collectives  8.19 us (9%)
  waiting for transfers between devices  2.32 us (2%)
    pallas_call x7, Pallas kernels, run(): pl.pallas_call(functools.partial(kernel, nodes), out_shape=[jax.ShapeDtyp...  52.1 us
    ppermute x6, starting transfers between devices, swapped(): return [lax.ppermute(v, 'space', q) for v, q in zip((first, second), pairs)]  12.4 us
    ppermute x4, starting transfers between devices, handed_on(): lax.ppermute(last, 'slab', [(i, i + 1) for i in range(k, peers - 1, 2)])  8.58 us
    all_gather x1, blocking collectives, body(): every = lax.all_gather(mine, 'slab', axis=0, tiled=True)  8.19 us
    unnamed x25, local copies, waits for them, and re-layouts  3.69 us
    reshape x1, local copies, waits for them, and re-layouts, body(): f = forcing.reshape(rows, elements)  2.73 us
    reshape x1, local copies, waits for them, and re-layouts, body(): return out.reshape(forcing.shape)  2.69 us
    ppermute x6, waiting for transfers between devices, swapped(): return [lax.ppermute(v, 'space', q) for v, q in zip((first, second), pairs)]  2.31 us
  transfers between devices with their start and end apart: 10, of which 1 were waited for; matrix products, arithmetic and copies ran while one was open for 1% of the time, Pallas kernels for 25%

commit v1 on v0

--- a/solution.py
+++ b/solution.py
@@ -13,7 +13,7 @@
 COARSE_UPWIND = 0.6
 F32 = jnp.float32
 BF16 = jnp.bfloat16
-VMEM_BYTES = 56 * 1024 * 1024
+VMEM_BYTES = 28 * 1024 * 1024
 
 
 def exact(a, b):
@@ -24,11 +24,59 @@
     return lax.broadcasted_iota(jnp.int32, shape, dim)
 
 
-def expand(small, rows, row_digit, cols, col_digit):
-    n, m = small.shape
-    left = (row_digit(iota((rows, n), 0)) == iota((rows, n), 1)).astype(F32)
-    right = (iota((m, cols), 0) == col_digit(iota((m, cols), 1))).astype(F32)
-    return exact(exact(left, small), right)
+def quotient(v, k):
+    if k & (k - 1) == 0:
+        return v >> (k.bit_length() - 1)
+    return v // k
+
+
+def digit(v, k, n):
+    return quotient(v, k) & (n - 1) if n & (n - 1) == 0 else quotient(v, k) % n
+
+
+def scalars(ref):
+    return [[ref[i, j] for j in range(ref.shape[1])] for i in range(ref.shape[0])]
+
+
+def two_minus(small):
+    return [[(2.0 if i == j else 0.0) - v for j, v in enumerate(row)] for i, row in enumerate(small)]
+
+
+def transposed(small):
+    return [list(row) for row in zip(*small)]
+
+
+def pick(at, values):
+    out = jnp.full(at.shape, values[-1], F32)
+    for k in range(len(values) - 2, -1, -1):
+        out = jnp.where(at == k, values[k], out)
+    return out
+
+
+def combine(left, rows):
+    outs = []
+    for line in left:
+        total = line[0] * rows[0]
+        for k in range(1, len(rows)):
+            total = total + line[k] * rows[k]
+        outs.append(total)
+    return outs
+
+
+def row_select(vectors, which, masks):
+    columns = vectors[0].shape[-1]
+    distinct = sorted(set(which))
+    out = jnp.broadcast_to(vectors[distinct[0]], (8, columns))
+    for v in distinct[1:]:
+        here = tuple(i for i in range(8) if which[i] == v)
+        if (here, columns) not in masks:
+            sub = iota((8, columns), 0)
+            mask = sub == here[0]
+            for i in here[1:]:
+                mask = jnp.logical_or(mask, sub == i)
+            masks[here, columns] = mask
+        out = jnp.where(masks[here, columns], vectors[v], out)
+    return out
 
 
 class Nodes:
@@ -37,81 +85,99 @@
         self.n = q * p**3
         self.nc = pc**3
         self.nf = 6 * pc**2
-
-    def fine(self, d):
-        p = self.p
-        if d == 0:
-            return lambda r: r // p**3
-        return lambda r: (r // p ** (3 - d)) % p
-
-    def coarse(self, d):
+        self.masks = {}
+
+    def fresh(self):
+        return Nodes(self.q, self.p, self.pc)
+
+    def fine(self, d, r):
+        return quotient(r, self.p**3) if d == 0 else digit(r, self.p ** (3 - d), self.p)
+
+    def coarse(self, d, r):
+        return digit(r, self.pc ** (3 - d), self.pc)
+
+    def bit(self, d, face, r):
         pc = self.pc
-        return lambda r: (r // pc ** (3 - d)) % pc
-
-    def face(self, r):
-        return r // self.pc**2
-
-    def bit(self, d, r):
-        pc = self.pc
-        high, low = (r // pc) % pc, r % pc
         if d == 1:
-            return high
+            return digit(r, pc, pc)
         if d == 3:
-            return low
-        return jnp.where(self.face(r) // 2 == 0, high, low)
-
-    def fine_fine(self, small, d):
-        return expand(small, self.n, self.fine(d), self.n, self.fine(d))
+            return digit(r, 1, pc)
+        return jnp.where(face < 2, digit(r, pc, pc), digit(r, 1, pc))
+
+    def over_fine(self, small, d):
+        at = self.fine(d, iota((1, self.n), 1))
+        return [pick(at, line) for line in small]
+
+    def over_coarse(self, small, d):
+        at = self.coarse(d, iota((1, self.nc), 1))
+        return [pick(at, line) for line in small]
+
+    def rows_of(self, count, factors):
+        parts = []
+        for g in range(0, count, 8):
+            total = None
+            for vectors, row_digit in factors:
+                term = row_select(vectors, [row_digit(g + i) for i in range(8)], self.masks)
+                total = term if total is None else total * term
+            parts.append(total)
+        return jnp.concatenate(parts, axis=0) if len(parts) > 1 else parts[0]
+
+    def fine_rows(self, time, x, y, z):
+        return self.rows_of(
+            self.n, [(v, functools.partial(self.fine, d)) for d, v in enumerate((time, x, y, z))]
+        )
+
+    def coarse_rows(self, time, x, y, z):
+        return self.rows_of(
+            self.nc,
+            [(time, lambda r: 0)] + [(v, functools.partial(self.coarse, d)) for d, v in ((1, x), (2, y), (3, z))],
+        )
 
     def kron(self, time, x, y, z):
-        return self.fine_fine(time, 0) * self.fine_fine(x, 1) * self.fine_fine(y, 2) * self.fine_fine(z, 3)
-
-    def restricted(self, time, x, y, z):
-        total = expand(time, self.nc, lambda r: r * 0, self.n, self.fine(0))
-        for d, small in ((1, x), (2, y), (3, z)):
-            total = total * expand(small, self.nc, self.coarse(d), self.n, self.fine(d))
-        return total
-
-    def prolonged(self, time_t, space_t):
-        total = expand(time_t, self.n, self.fine(0), self.nc, lambda r: r * 0)
+        return self.fine_rows(*(self.over_fine(v, d) for d, v in enumerate((time, x, y, z))))
+
+    def restricted(self, time, space):
+        return self.coarse_rows(*(self.over_fine(v, d) for d, v in enumerate((time, space, space, space))))
+
+    def prolonged(self, time, space):
+        ones = jnp.ones((1, self.nc), F32)
+        return self.fine_rows(
+            [ones * v for v in time[0]], *(self.over_coarse(transposed(space), d) for d in (1, 2, 3))
+        )
+
+    def coarse_coarse(self, small):
+        ones = [jnp.ones((1, self.nc), F32)]
+        return self.coarse_rows(ones, *(self.over_coarse(small, d) for d in (1, 2, 3)))
+
+    def face_traces(self, time, space):
+        four, pc, p = self.pc**2, self.pc, self.p
+        factors = [(self.over_fine(time, 0), lambda r: 0)]
         for d in (1, 2, 3):
-            total = total * expand(space_t, self.n, self.fine(d), self.nc, self.coarse(d))
-        return total
-
-    def coarse_coarse(self, small):
-        total = 1.0
+            at = self.fine(d, iota((1, self.n), 1))
+            vectors = self.over_fine(space, d)
+            vectors = vectors + [(at == node).astype(F32) for node in (p - 1, 0)]
+
+            def row_digit(r, d=d):
+                face, high, low = r // four, r // pc % pc, r % pc
+                if face // 2 == d - 1:
+                    return pc + face % 2
+                return high if d == 1 or (d == 2 and face < 2) else low
+
+            factors.append((vectors, row_digit))
+        return self.rows_of(self.nf, factors)
+
+    def face_spread(self, space):
+        col = iota((1, self.nf), 1)
+        face = quotient(col, self.pc**2)
+        factors = []
         for d in (1, 2, 3):
-            total = total * expand(small, self.nc, self.coarse(d), self.nc, self.coarse(d))
-        return total
-
-    def face_traces(self, time, space):
-        shape = (self.nf, self.n)
-        row, col = iota(shape, 0), iota(shape, 1)
-        face = self.face(row)
-        opposite = jnp.where(face % 2 == 0, self.p - 1, 0)
-        total = expand(time, self.nf, lambda r: r * 0, self.n, self.fine(0))
-        for d in (1, 2, 3):
-            tangential = expand(space, self.nf, functools.partial(self.bit, d), self.n, self.fine(d))
-            normal = (self.fine(d)(col) == opposite).astype(F32)
-            total = total * jnp.where(face // 2 == d - 1, normal, tangential)
-        return total
-
-    def face_spread(self, space):
-        shape = (self.nc, self.nf)
-        row, col = iota(shape, 0), iota(shape, 1)
-        face = self.face(col)
-        total = 1.0
-        node = lambda r: jnp.where(self.face(r) % 2 == 0, 0, self.p - 1)
-        for d in (1, 2, 3):
-            normal = expand(space, self.nc, self.coarse(d), self.nf, node)
-            tangential = (self.coarse(d)(row) == self.bit(d, col)).astype(F32)
-            total = total * jnp.where(face // 2 == d - 1, normal, tangential)
-        return total
-
-
-def two_minus(small):
-    n = small.shape[0]
-    return 2.0 * (iota((n, n), 0) == iota((n, n), 1)).astype(F32) - small
+            vectors = []
+            for i in range(self.pc):
+                normal = jnp.where(digit(face, 1, 2) == 0, space[i][0], space[i][self.p - 1])
+                tangential = (self.bit(d, face, col) == i).astype(F32)
+                vectors.append(jnp.where(quotient(face, 2) == d - 1, normal, tangential))
+            factors.append((vectors, functools.partial(self.coarse, d)))
+        return self.rows_of(self.nc, factors)
 
 
 def pieces(v):
@@ -214,36 +280,63 @@
     second_ref[...] = jnp.where(even, to_left, to_right)
 
 
-def start_kernel(nodes, parity, f_ref, c_ref, halo_ref, tb, sb, tr, sr, x_ref, first_ref, second_ref, last_ref, rf_ref):
+def inverse_of(nodes, tb, sb):
+    ti, si = two_minus(scalars(tb)), two_minus(scalars(sb))
+    return pieces(nodes.kron(ti, si, si, si))
+
+
+def from_halves(ref, row, p):
+    tiles = []
+    for k in range(0, ref.shape[1], 8):
+        first, second = ref[row, k : k + 8, :], ref[row + 1, k : k + 8, :]
+        low = lower_half(first.shape)
+        tiles.append(jnp.where(low, first, pltpu.roll(second, 4, 0)))
+        tiles.append(jnp.where(low, pltpu.roll(first, 4, 0), second))
+    return jnp.concatenate(tiles, axis=1)
+
+
+def to_halves(ref, row, values):
+    for k in range(0, ref.shape[1], 8):
+        at = 32 * k
+        first, second = values[:, at : at + 128], values[:, at + 128 : at + 256]
+        low = lower_half(first.shape)
+        ref[row, k : k + 8, :] = jnp.where(low, first, pltpu.roll(second, 4, 0))
+        ref[row + 1, k : k + 8, :] = jnp.where(low, pltpu.roll(first, 4, 0), second)
+
+
+def start_kernel(nodes, parity, tb, sb, tr, sr, f_ref, c_ref, halo_ref, x_ref, first_ref, second_ref, last_ref, rf_ref):
+    nodes = nodes.fresh()
     n, p = nodes.n, nodes.p
-    rows = f_ref.shape[0]
-    ti, si = two_minus(tb[...]), two_minus(sb[...])
-    inverse = pieces(nodes.kron(ti, si, si, si))
+    rows = x_ref.shape[0]
+    inverse = inverse_of(nodes, tb, sb)
     scale = 1.0 / c_ref[...]
     total = 0.0
     for s in range(rows // n):
-        f = f_ref[s * n : (s + 1) * n, :]
+        f = jnp.concatenate([from_halves(f_ref, (s * n + r) // p, p) for r in range(0, n, 8)], axis=0)
         total = total + f
         x_ref[s * n : (s + 1) * n, :] = product(inverse, pieces(f)) * scale
     pack(x_ref, halo_ref, parity, first_ref, second_ref, rows, p)
     at = rows - n + last_time(nodes)
     last_ref[...] = x_ref[at:rows, :]
-    rf_ref[...] = product(pieces(nodes.restricted(tr[...], sr[...], sr[...], sr[...])), pieces(total))
-
-
-def local_kernel(nodes, x_ref, x1_ref, c_ref, nb_ref, tb, sb, st, out_ref, g_ref, tiles_ref):
+    rf_ref[...] = product(pieces(nodes.restricted(scalars(tr), scalars(sr))), pieces(total))
+
+
+def local_kernel(nodes, tb, sb, st, x_ref, x1_ref, c_ref, nb_ref, out_ref, g_ref, tiles_ref):
+    nodes = nodes.fresh()
     n, p = nodes.n, nodes.p
     rows, elements = x_ref.shape
     plane = p**3
-    ti, si = two_minus(tb[...]), two_minus(sb[...])
-    tit, sis, sid = exact(ti, tb[...]), exact(si, sb[...]), exact(si, st[...])
-    et = nodes.fine_fine(ti, 0)
-    es = [nodes.fine_fine(si, d) for d in (1, 2, 3)]
-    ed = [nodes.fine_fine(sid, d) for d in (1, 2, 3)]
-    inverse = pieces(et * es[0] * es[1] * es[2])
+    t, b, d = scalars(tb), scalars(sb), scalars(st)
+    ti, si = two_minus(t), two_minus(b)
+    et = nodes.over_fine(ti, 0)
+    es = [nodes.over_fine(si, k) for k in (1, 2, 3)]
+    ed = [combine(si, nodes.over_fine(d, k)) for k in (1, 2, 3)]
+    eb = [combine(si, nodes.over_fine(b, k)) for k in (1, 2, 3)]
+    inverse = pieces(nodes.fine_rows(et, *es))
     unit = (iota((n, n), 0) == iota((n, n), 1)).astype(F32)
-    keep = pieces(unit - nodes.kron(tit, sis, sis, sis))
-    drift = pieces(-et * (ed[0] * es[1] * es[2] + es[0] * ed[1] * es[2] + es[0] * es[1] * ed[2]))
+    keep = pieces(unit - nodes.fine_rows(combine(ti, nodes.over_fine(t, 0)), *eb))
+    drift = nodes.fine_rows(et, ed[0], es[1], es[2]) + nodes.fine_rows(et, es[0], ed[1], es[2])
+    drift = pieces(-(drift + nodes.fine_rows(et, es[0], es[1], ed[2])))
     c = c_ref[...]
     scale = 1.0 / c
     g_ref[...] = jnp.zeros_like(g_ref)
@@ -275,11 +368,10 @@
     return jnp.where(even, second, first), jnp.where(even, first, second)
 
 
-def finish(nodes, parity, base_ref, got_first, got_second, prev_a, prev_b, c_ref, nb_ref, tb, sb, x_ref, g_ref):
+def finish(nodes, parity, tb, sb, base_ref, got_first, got_second, prev_a, prev_b, c_ref, nb_ref, x_ref, g_ref):
     n, p = nodes.n, nodes.p
     rows, elements = base_ref.shape
-    ti, si = two_minus(tb[...]), two_minus(sb[...])
-    inverse = pieces(nodes.kron(ti, si, si, si))
+    inverse = inverse_of(nodes, tb, sb)
     c = c_ref[...]
     scale = 1.0 / c
     left, right = ghosts(parity, got_first, got_second)
@@ -294,26 +386,32 @@
 
 
 def finish_kernel(
-    nodes, parity, base_ref, got_first, got_second, prev_a, prev_b, c_ref, nb_ref, halo_ref, tb, sb,
+    nodes, parity, tb, sb, base_ref, got_first, got_second, prev_a, prev_b, c_ref, nb_ref, halo_ref,
     x_ref, first_ref, second_ref, last_ref, g_ref,
 ):
-    finish(nodes, parity, base_ref, got_first, got_second, prev_a, prev_b, c_ref, nb_ref, tb, sb, x_ref, g_ref)
+    nodes = nodes.fresh()
+    finish(nodes, parity, tb, sb, base_ref, got_first, got_second, prev_a, prev_b, c_ref, nb_ref, x_ref, g_ref)
     rows = base_ref.shape[0]
     pack(x_ref, halo_ref, parity, first_ref, second_ref, rows, nodes.p)
     last_ref[...] = x_ref[rows - nodes.n + last_time(nodes) : rows, :]
 
 
 def coarse_kernel(
-    nodes, parity, base_ref, got_first, got_second, prev_a, prev_b, c_ref, nb_ref, halo_ref, rf_ref, tb, sb, st, tr, sr,
+    nodes, parity, tb, sb, st, tr, sr, base_ref, got_first, got_second, prev_a, prev_b, c_ref, nb_ref, halo_ref, rf_ref,
     x_ref, first_ref, second_ref, local_ref, g_ref,
 ):
-    finish(nodes, parity, base_ref, got_first, got_second, prev_a, prev_b, c_ref, nb_ref, tb, sb, x_ref, g_ref)
+    nodes = nodes.fresh()
+    finish(nodes, parity, tb, sb, base_ref, got_first, got_second, prev_a, prev_b, c_ref, nb_ref, x_ref, g_ref)
     n, p, nc = nodes.n, nodes.p, nodes.nc
     rows, elements = x_ref.shape
-    t, s = tr[...], sr[...]
-    tk, sk, sd = exact(t, tb[...]), exact(s, sb[...]), exact(s, st[...])
-    block = nodes.restricted(tk, sk, sk, sk)
-    stiff = nodes.restricted(t, sd, s, s) + nodes.restricted(t, s, sd, s) + nodes.restricted(t, s, s, sd)
+    t, s = scalars(tr), scalars(sr)
+    et = nodes.over_fine(t, 0)
+    es = [nodes.over_fine(s, k) for k in (1, 2, 3)]
+    ed = [combine(s, nodes.over_fine(scalars(st), k)) for k in (1, 2, 3)]
+    eb = [combine(s, nodes.over_fine(scalars(sb), k)) for k in (1, 2, 3)]
+    block = nodes.coarse_rows(combine(t, nodes.over_fine(scalars(tb), 0)), *eb)
+    stiff = nodes.coarse_rows(et, ed[0], es[1], es[2]) + nodes.coarse_rows(et, es[0], ed[1], es[2])
+    stiff = stiff + nodes.coarse_rows(et, es[0], es[1], ed[2])
     faces = nodes.face_traces(t, s)
     stacked = pieces(jnp.concatenate([block, stiff, faces], axis=0))
     total = x_ref[:n, :]
@@ -323,7 +421,7 @@
         at = (k - 1) * n + last_time(nodes)
         before = before + x_ref[at : at + p**3, :]
     applied = product(stacked, pieces(total))
-    first_node = pieces(nodes.restricted(t, s, s, s)[:, : p**3])
+    first_node = pieces(nodes.coarse_rows(et, *es)[:, : p**3])
     c = c_ref[...]
     local = rf_ref[...] - c * applied[:nc] - applied[nc : 2 * nc]
     local = local + (UPWIND * c) * product(first_node, pieces(before))
@@ -348,7 +446,8 @@
     second_ref[...] = jnp.where(even, to_left, to_right)
 
 
-def group_kernel(nodes, parity, local_ref, got_first, got_second, c_ref, nb_ref, sr, cs, out_ref):
+def group_kernel(nodes, parity, sr, cs, local_ref, got_first, got_second, c_ref, nb_ref, out_ref):
+    nodes = nodes.fresh()
     nc = nodes.nc
     elements = local_ref.shape[-1]
     left, right = ghosts(parity, got_first, got_second)
@@ -357,17 +456,18 @@
     from_right = select_columns(right, nb_ref[1:2, :] - (elements + count), count)
     low = iota((8, elements), 0) < nodes.pc**2
     both = jnp.where(low, from_left, from_right)
-    spread = nodes.face_spread(sr[...])[:, :8]
+    spread = nodes.face_spread(scalars(sr))[:, :8]
     scale = 1.0 / c_ref[...]
     total = (local_ref[:nc, :] + PENALTY * exact(spread, both)) * scale
-    smoother = nodes.coarse_coarse(cs[...])
+    smoother = nodes.coarse_coarse(scalars(cs))
     out_ref[:nc, :] = exact(smoother, total)
     out_ref[nc:, :] = exact(smoother, local_ref[nc:, :])
 
 
-def end_kernel(nodes, group, every_ref, x_ref, cs, trt, srt, out_ref):
-    nc, n = nodes.nc, nodes.n
-    transfer = COARSE_UPWIND * nodes.coarse_coarse(cs[...])
+def end_kernel(nodes, group, cs, tr, sr, every_ref, x_ref, out_ref):
+    nodes = nodes.fresh()
+    nc, n, p = nodes.nc, nodes.n, nodes.p
+    transfer = COARSE_UPWIND * nodes.coarse_coarse(scalars(cs))
     mine = group[0]
     peers = every_ref.shape[0] // (2 * nc)
     state = jnp.zeros((nc, x_ref.shape[-1]), F32)
@@ -377,17 +477,15 @@
         if g:
             after = after + every_ref[at - nc : at, :]
         state = jnp.where(g <= mine, after, state)
-    lifted = product(pieces(nodes.prolonged(trt[...], srt[...])), pieces(state))
-    for s in range(x_ref.shape[0] // n):
-        here = slice(s * n, (s + 1) * n)
-        out_ref[here, :] = x_ref[here, :] + lifted
-
-
-def call(kernel, nodes, outs, scratch=(), scalars=1):
-    smem = [pl.BlockSpec(memory_space=pltpu.SMEM)] * scalars
-
+    lifted = product(pieces(nodes.prolonged(scalars(tr), scalars(sr))), pieces(state))
+    for r in range(0, x_ref.shape[0], 8):
+        to_halves(out_ref, r // p, x_ref[r : r + 8, :] + lifted[r % n : r % n + 8, :])
+
+
+def call(kernel, nodes, outs, small, scratch=()):
     def run(*args):
-        in_specs = smem + [pl.BlockSpec(memory_space=pltpu.VMEM)] * (len(args) - scalars)
+        in_specs = [pl.BlockSpec(memory_space=pltpu.SMEM)] * len(small)
+        in_specs += [pl.BlockSpec(memory_space=pltpu.VMEM)] * len(args)
         return pl.pallas_call(
             functools.partial(kernel, nodes),
             out_shape=[jax.ShapeDtypeStruct(shape, F32) for shape in outs],
@@ -396,7 +494,7 @@
             scratch_shapes=[pltpu.VMEM(shape, F32) for shape in scratch],
             compiler_params=pltpu.CompilerParams(vmem_limit_bytes=VMEM_BYTES),
             name=kernel.__name__,
-        )(*args)
+        )(*small, *args)
 
     return run
 
@@ -423,7 +521,9 @@
     nodes = Nodes(q, p, space_restrict.shape[0])
     rows = slabs * nodes.n
     count = halo_faces.shape[-1]
-    f = forcing.reshape(rows, elements)
+    tiles = elements // 128
+    halves = (rows // p, tiles * p, 128)
+    f = forcing.reshape(rows // p, p, tiles, 128).transpose(0, 2, 1, 3).reshape(halves)
     c = coefficient.reshape(1, elements)
     parity = (lax.axis_index("space") % 2).astype(jnp.int32).reshape(1)
     group = lax.axis_index("slab").astype(jnp.int32).reshape(1)
@@ -431,34 +531,28 @@
     face = (rows // p, count)
     plane = (p**3, elements)
     nc = nodes.nc
-    x1, first, second, last, rf = call(start_kernel, nodes, (field, face, face, plane, (nc, elements)))(
-        parity, f, c, halo_faces, time_block, space_block, time_restrict, space_restrict
-    )
+    tb, sb, st, tr, sr, cs = time_block, space_block, stiffness, time_restrict, space_restrict, coarse_smoother
+    x1, first, second, last, rf = call(
+        start_kernel, nodes, (field, face, face, plane, (nc, elements)), (parity, tb, sb, tr, sr)
+    )(f, c, halo_faces)
     x = x1
     for sweep in range(SWEEPS - 1):
         got = swapped(first, second) + handed_on(last)
-        (base,) = call(local_kernel, nodes, (field,), (field, (elements // 128, rows, 128)), 0)(
-            x, x1, c, neighbours, time_block, space_block, stiffness
-        )
+        (base,) = call(local_kernel, nodes, (field,), (tb, sb, st), (field, (tiles, rows, 128)))(x, x1, c, neighbours)
         if sweep < SWEEPS - 2:
-            x, first, second, last = call(finish_kernel, nodes, (field, face, face, plane), (field,))(
-                parity, base, *got, c, neighbours, halo_faces, time_block, space_block
-            )
+            x, first, second, last = call(
+                finish_kernel, nodes, (field, face, face, plane), (parity, tb, sb), (field,)
+            )(base, *got, c, neighbours, halo_faces)
         else:
             x, first, second, local = call(
-                coarse_kernel, nodes, (field, (8, count), (8, count), (2 * nc, elements)), (field,)
-            )(
-                parity, base, *got, c, neighbours, halo_faces, rf, time_block, space_block, stiffness,
-                time_restrict, space_restrict,
-            )
+                coarse_kernel, nodes, (field, (8, count), (8, count), (2 * nc, elements)),
+                (parity, tb, sb, st, tr, sr), (field,),
+            )(base, *got, c, neighbours, halo_faces, rf)
     got = swapped(first, second)
-    (mine,) = call(group_kernel, nodes, ((2 * nc, elements),))(
-        parity, local, *got, c, neighbours, space_restrict, coarse_smoother
-    )
+    (mine,) = call(group_kernel, nodes, ((2 * nc, elements),), (parity, sr, cs))(local, *got, c, neighbours)
     every = lax.all_gather(mine, "slab", axis=0, tiled=True)
-    (out,) = call(end_kernel, nodes, (field,))(
-        group, every, x, coarse_smoother, time_restrict.T, space_restrict.T
-    )
+    (out,) = call(end_kernel, nodes, (halves,), (group, cs, tr, sr))(every, x)
+    out = out.reshape(rows // p, tiles, p, 128).transpose(0, 2, 1, 3)
     return out.reshape(forcing.shape)
 
 

time: 94.1 us -> 65.5 us (0.70)
  Pallas kernels: 52.1 us -> 26.8 us
  local copies, waits for them, and re-layouts: 9.79 us -> 5.52 us
  waiting for transfers between devices: 2.32 us -> 3.46 us
    pallas_call x7, Pallas kernels: 52.1 us -> 26.8 us  [run(): pl.pallas_call(functools.partial(kernel, nodes), out_shape=[jax.ShapeDtyp...]
    reshape x2 -> x0, local copies, waits for them, and re-layouts: 5.42 us -> none  [the longest x1 2.73 us: body(): f = forcing.reshape(rows, elements)]
    unnamed x25 -> x30, local copies, waits for them, and re-layouts: 3.69 us -> 5.52 us
    ppermute x6, waiting for transfers between devices: 2.31 us -> 3.45 us  [swapped(): return [lax.ppermute(v, 'space', q) for v, q in zip((first, second), pairs)]]
  transfers between devices with their start and end apart: 10 -> 10, of which waited for: 1 -> 1; matrix products, arithmetic and copies ran while one was open for 1% -> 0% of each run, Pallas kernels for 25% -> 19%
where the time goes in v1:
time: 65.5 us; the launch traced here: 65.1 us
  Pallas kernels  26.8 us (41%)
  starting transfers between devices  20.4 us (31%)
  blocking collectives  8.74 us (13%)
  local copies, waits for them, and re-layouts  5.52 us (8%)
  waiting for transfers between devices  3.46 us (5%)
    pallas_call x7, Pallas kernels, run(): pl.pallas_call(functools.partial(kernel, nodes), out_shape=[jax.ShapeDtyp...  26.8 us
    ppermute x6, starting transfers between devices, swapped(): return [lax.ppermute(v, 'space', q) for v, q in zip((first, second), pairs)]  12.1 us
    all_gather x1, blocking collectives, body(): every = lax.all_gather(mine, 'slab', axis=0, tiled=True)  8.74 us
    ppermute x4, starting transfers between devices, handed_on(): lax.ppermute(last, 'slab', [(i, i + 1) for i in range(k, peers - 1, 2)])  8.23 us
    unnamed x30, local copies, waits for them, and re-layouts  5.52 us
    ppermute x6, waiting for transfers between devices, swapped(): return [lax.ppermute(v, 'space', q) for v, q in zip((first, second), pairs)]  3.45 us
  transfers between devices with their start and end apart: 10, of which 1 were waited for; matrix products, arithmetic and copies ran while one was open for 0% of the time, Pallas kernels for 19%

profile of v1, /device:TPU:9, one launch (start us, length us, event | category | flops | bytes accessed | tf_op | source)
XLA Modules:
  0.0 65.1 jit_solution(9135612968937240545)
XLA Ops:
  0.0 1.4 %copy-done = f32[2,3,4,4,4,1024]{5,4,3,2,1,0:T(4,128)S(1)} copy-done((f32[2,3,4,4,4,1024]{5,4,3,2,1,0:T(4,128)S(1)}, f32[2,3,4,4,4,1024]{5,4,3,2,1,0:T(4,128)}, u32[]{:S(2)}) %copy-start) | copy-done | bytes 1572888
  1.4 0.7 %copy-done.2 = f32[1024]{0:T(1024)S(1)} copy-done((f32[1024]{0:T(1024)S(1)}, f32[1024]{0:T(1024)}, u32[]{:S(2)}) %copy-start.2) | copy-done | bytes 4120
  2.1 0.7 %copy-done.4 = f32[3,3]{1,0:T(4,128)S(1)} copy-done((f32[3,3]{1,0:T(4,128)S(1)}, f32[3,3]{1,0:T(4,128)}, u32[]{:S(2)}) %copy-start.4) | copy-done | bytes 60
  2.8 0.7 %copy-done.6 = f32[4,4]{1,0:T(4,128)S(1)} copy-done((f32[4,4]{1,0:T(4,128)S(1)}, f32[4,4]{1,0:T(4,128)}, u32[]{:S(2)}) %copy-start.6) | copy-done | bytes 88
  3.5 0.7 %copy-done.7 = s32[2,512]{1,0:T(2,128)S(1)} copy-done((s32[2,512]{1,0:T(2,128)S(1)}, s32[2,512]{1,0:T(2,128)}, u32[]{:S(2)}) %copy-start.7) | copy-done | bytes 4120
  5.5 2.2 %start_kernel.1 = (f32[384,1024]{1,0:T(8,128)S(1)}, f32[96,512]{1,0:T(8,128)S(1)}, f32[96,512]{1,0:T(8,128)S(1)}, f32[64,1024]{1,0:T(8,128)S(1)}, f32[8,1024]{1,0:T(8,128)S(1)}) custom-call(s32[1]{0:T(128)} %bitcast.1.parity, f32[3,3]{1,0:T(4,128)S(1)} %copy-done.4, f32[4,4]{1,0:T(4,128)S(1)} %copy-done.6, f32[1,3]{1,0:T(1,128)S(1)} %copy-done.12, ...), custom_call_target="tpu_custom_call" | custom-call | tf_op jit(solution)/shard_map/start_kernel/pallas_call | solution.py:489
  7.7 3.7 %collective-permute-start.3 = (f32[64,1024]{1,0:T(8,128)S(1)}, f32[64,1024]{1,0:T(8,128)S(1)}, u32[]{:S(2)}, u32[]{:S(2)}) collective-permute-start(f32[64,1024]{1,0:T(8,128)S(1)} %get-tuple-element.21), channel_id=1, source_target_pairs={{8,16},{9,17},{10,18},{11,19},{12,20},{13,21},{14,22},{15,23}} | collective-permute-start | bytes 786440 | tf_op jit(solution)/shard_map/ppermute | solution.py:512
  11.4 1.3 %collective-permute-start.2 = (f32[64,1024]{1,0:T(8,128)S(1)}, f32[64,1024]{1,0:T(8,128)S(1)}, u32[]{:S(2)}, u32[]{:S(2)}) collective-permute-start(f32[64,1024]{1,0:T(8,128)S(1)} %get-tuple-element.21), channel_id=1, source_target_pairs={{0,8},{16,24},{1,9},{17,25},{2,10},{18,26},{3,11},{19,27},{4,12},{... | collective-permute-start | bytes 786440 | tf_op jit(solution)/shard_map/ppermute | solution.py:512
  12.7 1.3 %collective-permute-start = (f32[96,512]{1,0:T(8,128)S(1)}, f32[96,512]{1,0:T(8,128)S(1)}, u32[]{:S(2)}, u32[]{:S(2)}) collective-permute-start(f32[96,512]{1,0:T(8,128)S(1)} %get-tuple-element.19), channel_id=1, source_target_pairs={{0,1},{1,0},{2,3},{3,2},{4,5},{5,4},{6,7},{7,6},{8,9},{9,8},{10,11... | collective-permute-start | bytes 589832 | tf_op jit(solution)/shard_map/ppermute | solution.py:507
  14.0 2.0 %collective-permute-start.1 = (f32[96,512]{1,0:T(8,128)S(1)}, f32[96,512]{1,0:T(8,128)S(1)}, u32[]{:S(2)}, u32[]{:S(2)}) collective-permute-start(f32[96,512]{1,0:T(8,128)S(1)} %get-tuple-element.20), channel_id=1, source_target_pairs={{1,2},{2,1},{3,4},{4,3},{5,6},{6,5},{9,10},{10,9},{11,12},{12,11},... | collective-permute-start | bytes 589832 | tf_op jit(solution)/shard_map/ppermute | solution.py:507
  16.1 6.2 %local_kernel.2.base_ref = f32[384,1024]{1,0:T(8,128)S(1)} custom-call(f32[3,3]{1,0:T(4,128)S(1)} %copy-done.5, f32[4,4]{1,0:T(4,128)S(1)} %copy-done.6, f32[4,4]{1,0:T(4,128)S(1)} %copy-done.9, f32[384,1024]{1,0:T(8,128)S(1)} %get-tuple-element.18.x_ref.x1_ref, f32[384,1024]{1,0:T(8,128)S(1)} %get-tuple-element.18.x_ref.x1_ref, f32[1,1024]{1,0:T(1,128)S(1)} %bitcast.15, ...), custom_call_target="tpu_custom_call" | custom-call | tf_op jit(solution)/shard_map/local_kernel/pallas_call | solution.py:489
  22.4 2.6 %finish_kernel.1 = (f32[384,1024]{1,0:T(8,128)S(1)}, f32[96,512]{1,0:T(8,128)S(1)}, f32[96,512]{1,0:T(8,128)S(1)}, f32[64,1024]{1,0:T(8,128)S(1)}) custom-call(s32[1]{0:T(128)} %bitcast.1.parity, f32[3,3]{1,0:T(4,128)S(1)} %copy-done.5, f32[4,4]{1,0:T(4,128)S(1)} %copy-done.6, f32[384,1024]{1,0:T(8,128)S(1)} %local_kernel.2.base_ref, ...), custom_call_target="tpu_custom_call" | custom-call | tf_op jit(solution)/shard_map/finish_kernel/pallas_call | solution.py:489
  25.0 2.0 %collective-permute-start.7 = (f32[64,1024]{1,0:T(8,128)S(1)}, f32[64,1024]{1,0:T(8,128)S(1)}, u32[]{:S(2)}, u32[]{:S(2)}) collective-permute-start(f32[64,1024]{1,0:T(8,128)S(1)} %get-tuple-element.25), channel_id=1, source_target_pairs={{8,16},{9,17},{10,18},{11,19},{12,20},{13,21},{14,22},{15,23}} | collective-permute-start | bytes 786440 | tf_op jit(solution)/shard_map/ppermute | solution.py:512
  27.0 1.3 %collective-permute-start.6 = (f32[64,1024]{1,0:T(8,128)S(1)}, f32[64,1024]{1,0:T(8,128)S(1)}, u32[]{:S(2)}, u32[]{:S(2)}) collective-permute-start(f32[64,1024]{1,0:T(8,128)S(1)} %get-tuple-element.25), channel_id=1, source_target_pairs={{0,8},{16,24},{1,9},{17,25},{2,10},{18,26},{3,11},{19,27},{4,12},{... | collective-permute-start | bytes 786440 | tf_op jit(solution)/shard_map/ppermute | solution.py:512
  28.3 2.3 %collective-permute-start.4 = (f32[96,512]{1,0:T(8,128)S(1)}, f32[96,512]{1,0:T(8,128)S(1)}, u32[]{:S(2)}, u32[]{:S(2)}) collective-permute-start(f32[96,512]{1,0:T(8,128)S(1)} %get-tuple-element.23), channel_id=1, source_target_pairs={{0,1},{1,0},{2,3},{3,2},{4,5},{5,4},{6,7},{7,6},{8,9},{9,8},{10,11... | collective-permute-start | bytes 589832 | tf_op jit(solution)/shard_map/ppermute | solution.py:507
  30.6 2.1 %collective-permute-start.5 = (f32[96,512]{1,0:T(8,128)S(1)}, f32[96,512]{1,0:T(8,128)S(1)}, u32[]{:S(2)}, u32[]{:S(2)}) collective-permute-start(f32[96,512]{1,0:T(8,128)S(1)} %get-tuple-element.24), channel_id=1, source_target_pairs={{1,2},{2,1},{3,4},{4,3},{5,6},{6,5},{9,10},{10,9},{11,12},{12,11},... | collective-permute-start | bytes 589832 | tf_op jit(solution)/shard_map/ppermute | solution.py:507
  32.7 6.2 %local_kernel.3.base_ref = f32[384,1024]{1,0:T(8,128)S(1)} custom-call(f32[3,3]{1,0:T(4,128)S(1)} %copy-done.5, f32[4,4]{1,0:T(4,128)S(1)} %copy-done.6, f32[4,4]{1,0:T(4,128)S(1)} %copy-done.9, f32[384,1024]{1,0:T(8,128)S(1)} %get-tuple-element.22.x_ref, f32[384,1024]{1,0:T(8,128)S(1)} %get-tuple-element.18.x_ref.x1_ref, f32[1,1024]{1,0:T(1,128)S(1)} %bitcast.17, ...), custom_call_target="tpu_custom_call" | custom-call | tf_op jit(solution)/shard_map/local_kernel/pallas_call | solution.py:489
  39.0 5.4 %coarse_kernel.1 = (f32[384,1024]{1,0:T(8,128)S(1)}, f32[8,512]{1,0:T(8,128)S(1)}, f32[8,512]{1,0:T(8,128)S(1)}, f32[16,1024]{1,0:T(8,128)S(1)}) custom-call(s32[1]{0:T(128)} %bitcast.1.parity, f32[3,3]{1,0:T(4,128)S(1)} %copy-done.5, f32[4,4]{1,0:T(4,128)S(1)} %copy-done.6, f32[4,4]{1,0:T(4,128)S(1)} %copy-done.9, f32[1,3]{1,0:T(1,128)S(1)} %copy-done.12, ...), custom_call_target="tpu_custom_call" | custom-call | tf_op jit(solution)/shard_map/coarse_kernel/pallas_call | solution.py:489
  44.4 2.5 %collective-permute-start.8 = (f32[8,512]{1,0:T(8,128)S(1)}, f32[8,512]{1,0:T(8,128)S(1)}, u32[]{:S(2)}, u32[]{:S(2)}) collective-permute-start(f32[8,512]{1,0:T(8,128)S(1)} %get-tuple-element.28), channel_id=1, source_target_pairs={{0,1},{1,0},{2,3},{3,2},{4,5},{5,4},{6,7},{7,6},{8,9},{9,8},{10,11... | collective-permute-start | bytes 49160 | tf_op jit(solution)/shard_map/ppermute | solution.py:507
  46.9 1.9 %collective-permute-start.9 = (f32[8,512]{1,0:T(8,128)S(1)}, f32[8,512]{1,0:T(8,128)S(1)}, u32[]{:S(2)}, u32[]{:S(2)}) collective-permute-start(f32[8,512]{1,0:T(8,128)S(1)} %get-tuple-element.29), channel_id=1, source_target_pairs={{1,2},{2,1},{3,4},{4,3},{5,6},{6,5},{9,10},{10,9},{11,12},{12,11},... | collective-permute-start | bytes 49160 | tf_op jit(solution)/shard_map/ppermute | solution.py:507
  48.8 3.4 %collective-permute-done.9.got_second = f32[8,512]{1,0:T(8,128)S(1)} collective-permute-done((f32[8,512]{1,0:T(8,128)S(1)}, f32[8,512]{1,0:T(8,128)S(1)}, u32[]{:S(2)}, u32[]{:S(2)}) %collective-permute-start.9) | collective-permute-done | bytes 16416 | tf_op jit(solution)/shard_map/ppermute | solution.py:507
  52.3 1.3 %group_kernel.1 = f32[16,1024]{1,0:T(8,128)S(1)} custom-call(s32[1]{0:T(128)} %bitcast.1.parity, f32[2,4]{1,0:T(2,128)S(1)} %copy-done.11, f32[2,2]{1,0:T(2,128)S(1)} %copy-done.14, f32[16,1024]{1,0:T(8,128)S(1)} %get-tuple-element.27.local_ref, f32[8,512]{1,0:T(8,128)S(1)} %collective-permute-done.8.got_first, ...), custom_call_target="tpu_custom_call" | custom-call | tf_op jit(solution)/shard_map/group_kernel/pallas_call | solution.py:489
  53.6 8.7 %all_gather.3.every_ref = f32[64,1024]{1,0:T(8,128)S(1)} all-gather(f32[16,1024]{1,0:T(8,128)S(1)} %group_kernel.1), channel_id=1, replica_groups=mesh['slab'=4,'space'=8] {'slab'}, dimensions={0}, use_global_device_ids=true | all-gather | bytes 327680 | tf_op jit(solution)/shard_map/all_gather | solution.py:553
  62.3 2.8 %end_kernel.1 = f32[96,32,128]{2,1,0:T(8,128)} custom-call(s32[1]{0:T(128)} %bitcast.group, f32[2,2]{1,0:T(2,128)S(1)} %copy-done.14, f32[1,3]{1,0:T(1,128)S(1)} %copy-done.13, f32[2,4]{1,0:T(2,128)S(1)} %copy-done.11, f32[64,1024]{1,0:T(8,128)S(1)} %all_gather.3.every_ref, f32[384,1024]{1,0:T(8,128)S(1)} %get-tuple-element.30.x_ref), custom_call_target="tpu_custom_call" | custom-call | tf_op jit(solution)/shard_map/end_kernel/pallas_call | solution.py:489
  (34 shorter events, 1.4 us)
Async XLA Ops:
  0.0 16.1 %copy-start.1 = (s32[6,1024]{1,0:T(8,128)S(1)}, s32[6,1024]{1,0:T(8,128)}, u32[]{:S(2)}) copy-start(s32[6,1024]{1,0:T(8,128)} %nb_ref.9) | copy-start | bytes 73732
  0.0 1.4 %copy-start = (f32[2,3,4,4,4,1024]{5,4,3,2,1,0:T(4,128)S(1)}, f32[2,3,4,4,4,1024]{5,4,3,2,1,0:T(4,128)}, u32[]{:S(2)}) copy-start(f32[2,3,4,4,4,1024]{5,4,3,2,1,0:T(4,128)} %param.10) | copy-start | bytes 4718596
  1.4 0.7 %copy-start.2 = (f32[1024]{0:T(1024)S(1)}, f32[1024]{0:T(1024)}, u32[]{:S(2)}) copy-start(f32[1024]{0:T(1024)} %param.11) | copy-start | bytes 12292
  2.1 0.7 %copy-start.4 = (f32[3,3]{1,0:T(4,128)S(1)}, f32[3,3]{1,0:T(4,128)}, u32[]{:S(2)}) copy-start(f32[3,3]{1,0:T(4,128)} %tb.9) | copy-start | bytes 112
  2.8 0.7 %copy-start.6 = (f32[4,4]{1,0:T(4,128)S(1)}, f32[4,4]{1,0:T(4,128)}, u32[]{:S(2)}) copy-start(f32[4,4]{1,0:T(4,128)} %sb.9) | copy-start | bytes 196
  3.5 0.7 %copy-start.7 = (s32[2,512]{1,0:T(2,128)S(1)}, s32[2,512]{1,0:T(2,128)}, u32[]{:S(2)}) copy-start(s32[2,512]{1,0:T(2,128)} %halo_ref.5) | copy-start | bytes 12292
  4.2 0.7 %copy-start.10 = (f32[2,4]{1,0:T(2,128)S(1)}, f32[2,4]{1,0:T(2,128)}, u32[]{:S(2)}) copy-start(f32[2,4]{1,0:T(2,128)} %sr.7) | copy-start | bytes 100
  5.5 10.6 %copy-start.3 = (f32[1024]{0:T(1024)S(1)}, f32[1024]{0:T(1024)}, u32[]{:S(2)}) copy-start(f32[1024]{0:T(1024)} %param.11) | copy-start | bytes 12292
  5.5 10.6 %copy-start.5 = (f32[3,3]{1,0:T(4,128)S(1)}, f32[3,3]{1,0:T(4,128)}, u32[]{:S(2)}) copy-start(f32[3,3]{1,0:T(4,128)} %tb.9) | copy-start | bytes 112
  5.5 10.6 %copy-start.9 = (f32[4,4]{1,0:T(4,128)S(1)}, f32[4,4]{1,0:T(4,128)}, u32[]{:S(2)}) copy-start(f32[4,4]{1,0:T(4,128)} %st.5) | copy-start | bytes 196
  7.7 14.6 %collective-permute-start.3 = (f32[64,1024]{1,0:T(8,128)S(1)}, f32[64,1024]{1,0:T(8,128)S(1)}, u32[]{:S(2)}, u32[]{:S(2)}) collective-permute-start(f32[64,1024]{1,0:T(8,128)S(1)} %get-tuple-element.21), channel_id=1, source_target_pairs={{8,16},{9,17},{10,18},{11,19},{12,20},{13,21},{14,22},{15,23}} | collective-permute-start | bytes 786440 | tf_op jit(solution)/shard_map/ppermute | solution.py:512
  11.4 10.9 %collective-permute-start.2 = (f32[64,1024]{1,0:T(8,128)S(1)}, f32[64,1024]{1,0:T(8,128)S(1)}, u32[]{:S(2)}, u32[]{:S(2)}) collective-permute-start(f32[64,1024]{1,0:T(8,128)S(1)} %get-tuple-element.21), channel_id=1, source_target_pairs={{0,8},{16,24},{1,9},{17,25},{2,10},{18,26},{3,11},{19,27},{4,12},{... | collective-permute-start | bytes 786440 | tf_op jit(solution)/shard_map/ppermute | solution.py:512
  12.7 9.6 %collective-permute-start = (f32[96,512]{1,0:T(8,128)S(1)}, f32[96,512]{1,0:T(8,128)S(1)}, u32[]{:S(2)}, u32[]{:S(2)}) collective-permute-start(f32[96,512]{1,0:T(8,128)S(1)} %get-tuple-element.19), channel_id=1, source_target_pairs={{0,1},{1,0},{2,3},{3,2},{4,5},{5,4},{6,7},{7,6},{8,9},{9,8},{10,11... | collective-permute-start | bytes 589832 | tf_op jit(solution)/shard_map/ppermute | solution.py:507
  14.0 8.3 %collective-permute-start.1 = (f32[96,512]{1,0:T(8,128)S(1)}, f32[96,512]{1,0:T(8,128)S(1)}, u32[]{:S(2)}, u32[]{:S(2)}) collective-permute-start(f32[96,512]{1,0:T(8,128)S(1)} %get-tuple-element.20), channel_id=1, source_target_pairs={{1,2},{2,1},{3,4},{4,3},{5,6},{6,5},{9,10},{10,9},{11,12},{12,11},... | collective-permute-start | bytes 589832 | tf_op jit(solution)/shard_map/ppermute | solution.py:507
  16.1 6.3 %copy-start.8 = (s32[2,512]{1,0:T(2,128)S(1)}, s32[2,512]{1,0:T(2,128)}, u32[]{:S(2)}) copy-start(s32[2,512]{1,0:T(2,128)} %halo_ref.5) | copy-start | bytes 12292
  25.0 14.0 %collective-permute-start.7 = (f32[64,1024]{1,0:T(8,128)S(1)}, f32[64,1024]{1,0:T(8,128)S(1)}, u32[]{:S(2)}, u32[]{:S(2)}) collective-permute-start(f32[64,1024]{1,0:T(8,128)S(1)} %get-tuple-element.25), channel_id=1, source_target_pairs={{8,16},{9,17},{10,18},{11,19},{12,20},{13,21},{14,22},{15,23}} | collective-permute-start | bytes 786440 | tf_op jit(solution)/shard_map/ppermute | solution.py:512
  27.0 12.0 %collective-permute-start.6 = (f32[64,1024]{1,0:T(8,128)S(1)}, f32[64,1024]{1,0:T(8,128)S(1)}, u32[]{:S(2)}, u32[]{:S(2)}) collective-permute-start(f32[64,1024]{1,0:T(8,128)S(1)} %get-tuple-element.25), channel_id=1, source_target_pairs={{0,8},{16,24},{1,9},{17,25},{2,10},{18,26},{3,11},{19,27},{4,12},{... | collective-permute-start | bytes 786440 | tf_op jit(solution)/shard_map/ppermute | solution.py:512
  28.3 10.7 %collective-permute-start.4 = (f32[96,512]{1,0:T(8,128)S(1)}, f32[96,512]{1,0:T(8,128)S(1)}, u32[]{:S(2)}, u32[]{:S(2)}) collective-permute-start(f32[96,512]{1,0:T(8,128)S(1)} %get-tuple-element.23), channel_id=1, source_target_pairs={{0,1},{1,0},{2,3},{3,2},{4,5},{5,4},{6,7},{7,6},{8,9},{9,8},{10,11... | collective-permute-start | bytes 589832 | tf_op jit(solution)/shard_map/ppermute | solution.py:507
  30.6 8.4 %collective-permute-start.5 = (f32[96,512]{1,0:T(8,128)S(1)}, f32[96,512]{1,0:T(8,128)S(1)}, u32[]{:S(2)}, u32[]{:S(2)}) collective-permute-start(f32[96,512]{1,0:T(8,128)S(1)} %get-tuple-element.24), channel_id=1, source_target_pairs={{1,2},{2,1},{3,4},{4,3},{5,6},{6,5},{9,10},{10,9},{11,12},{12,11},... | collective-permute-start | bytes 589832 | tf_op jit(solution)/shard_map/ppermute | solution.py:507
  39.0 13.3 %copy-start.11 = (f32[2,4]{1,0:T(2,128)S(1)}, f32[2,4]{1,0:T(2,128)}, u32[]{:S(2)}) copy-start(f32[2,4]{1,0:T(2,128)} %sr.7) | copy-start | bytes 100
  39.0 13.3 %copy-start.14 = (f32[2,2]{1,0:T(2,128)S(1)}, f32[2,2]{1,0:T(2,128)}, u32[]{:S(2)}) copy-start(f32[2,2]{1,0:T(2,128)} %cs.3) | copy-start | bytes 52
  39.0 23.3 %copy-start.13 = (f32[1,3]{1,0:T(1,128)S(1)}, f32[1,3]{1,0:T(1,128)}, u32[]{:S(2)}) copy-start(f32[1,3]{1,0:T(1,128)} %tr.5) | copy-start | bytes 40
  44.4 4.4 %collective-permute-start.8 = (f32[8,512]{1,0:T(8,128)S(1)}, f32[8,512]{1,0:T(8,128)S(1)}, u32[]{:S(2)}, u32[]{:S(2)}) collective-permute-start(f32[8,512]{1,0:T(8,128)S(1)} %get-tuple-element.28), channel_id=1, source_target_pairs={{0,1},{1,0},{2,3},{3,2},{4,5},{5,4},{6,7},{7,6},{8,9},{9,8},{10,11... | collective-permute-start | bytes 49160 | tf_op jit(solution)/shard_map/ppermute | solution.py:507
  46.9 5.4 %collective-permute-start.9 = (f32[8,512]{1,0:T(8,128)S(1)}, f32[8,512]{1,0:T(8,128)S(1)}, u32[]{:S(2)}, u32[]{:S(2)}) collective-permute-start(f32[8,512]{1,0:T(8,128)S(1)} %get-tuple-element.29), channel_id=1, source_target_pairs={{1,2},{2,1},{3,4},{4,3},{5,6},{6,5},{9,10},{10,9},{11,12},{12,11},... | collective-permute-start | bytes 49160 | tf_op jit(solution)/shard_map/ppermute | solution.py:507
  (1 other events, 0.7 us)

commit v2 on v1

v2 whole, which is shorter than its diff:
```python
import functools

import jax
import jax.numpy as jnp
from jax import lax
from jax.experimental import pallas as pl
from jax.experimental.pallas import tpu as pltpu
from jax.sharding import PartitionSpec as P

SWEEPS = 3
PENALTY = 0.3
UPWIND = 0.5
COARSE_UPWIND = 0.6
F32 = jnp.float32
BF16 = jnp.bfloat16
VMEM_BYTES = 28 * 1024 * 1024


def iota(shape, dim):
    return lax.broadcasted_iota(jnp.int32, shape, dim)


def quotient(v, k):
    if k & (k - 1) == 0:
        return v >> (k.bit_length() - 1)
    return v // k


def digit(v, k, n):
    return quotient(v, k) & (n - 1) if n & (n - 1) == 0 else quotient(v, k) % n


def scalars(ref):
    return [[ref[i, j] for j in range(ref.shape[1])] for i in range(ref.shape[0])]


def two_minus(small):
    return [[(2.0 if i == j else 0.0) - v for j, v in enumerate(row)] for i, row in enumerate(small)]


def transposed(small):
    return [list(row) for row in zip(*small)]


def small_product(a, b):
    return [[sum(a[i][k] * b[k][j] for k in range(len(b))) for j in range(len(b[0]))] for i in range(len(a))]


def pick(at, values):
    out = jnp.zeros(at.shape, F32) + values[-1]
    for k in range(len(values) - 2, -1, -1):
        out = jnp.where(at == k, values[k], out)
    return out


def combine(left, rows):
    outs = []
    for line in left:
        total = line[0] * rows[0]
        for k in range(1, len(rows)):
            total = total + line[k] * rows[k]
        outs.append(total)
    return outs


def row_select(vectors, which, masks):
    columns = vectors[0].shape[-1]
    distinct = sorted(set(which))
    out = jnp.broadcast_to(vectors[distinct[0]], (8, columns))
    for v in distinct[1:]:
        here = tuple(i for i in range(8) if which[i] == v)
        if (here, columns) not in masks:
            sub = iota((8, columns), 0)
            mask = sub == here[0]
            for i in here[1:]:
                mask = jnp.logical_or(mask, sub == i)
            masks[here, columns] = mask
        out = jnp.where(masks[here, columns], vectors[v], out)
    return out


class Nodes:
    def __init__(self, q, p, pc):
        self.q, self.p, self.pc = q, p, pc
        self.n = q * p**3
        self.nc = pc**3
        self.nf = 6 * pc**2
        self.masks = {}

    def fresh(self):
        return Nodes(self.q, self.p, self.pc)

    def fine(self, d, r):
        return quotient(r, self.p**3) if d == 0 else digit(r, self.p ** (3 - d), self.p)

    def coarse(self, d, r):
        return digit(r, self.pc ** (3 - d), self.pc)

    def bit(self, d, face, r):
        pc = self.pc
        if d == 1:
            return digit(r, pc, pc)
        if d == 3:
            return digit(r, 1, pc)
        return jnp.where(face < 2, digit(r, pc, pc), digit(r, 1, pc))

    def over_fine(self, small, d):
        at = self.fine(d, iota((1, self.n), 1))
        return [pick(at, line) for line in small]

    def rows_of(self, count, factors):
        parts = []
        for g in range(0, count, 8):
            total = None
            for vectors, row_digit in factors:
                term = row_select(vectors, [row_digit(g + i) for i in range(8)], self.masks)
                total = term if total is None else total * term
            parts.append(total)
        return jnp.concatenate(parts, axis=0) if len(parts) > 1 else parts[0]

    def fine_rows(self, time, x, y, z):
        return self.rows_of(
            self.n, [(v, functools.partial(self.fine, d)) for d, v in enumerate((time, x, y, z))]
        )

    def coarse_rows(self, time, x, y, z):
        return self.rows_of(
            self.nc,
            [(time, lambda r: 0)] + [(v, functools.partial(self.coarse, d)) for d, v in ((1, x), (2, y), (3, z))],
        )

    def kron(self, time, x, y, z):
        return self.fine_rows(*(self.over_fine(v, d) for d, v in enumerate((time, x, y, z))))

    def restricted(self, time, space):
        return self.coarse_rows(*(self.over_fine(v, d) for d, v in enumerate((time, space, space, space))))

    def lifted(self, time, space, smoother, mine, sources):
        width = 2 * self.nc
        col = iota((1, width * len(sources)), 1)
        block = quotient(col, width)
        owner = jnp.zeros_like(col) + sources[0]
        for k in range(1, len(sources)):
            owner = jnp.where(block == k, sources[k], owner)
        steps = mine - owner - digit(col, self.nc, 2)
        power, decay, powers, decays = smoother, 1.0, [], []
        for _ in sources:
            powers.append(small_product(transposed(space), power))
            decays.append(decay)
            power, decay = small_product(power, smoother), decay * COARSE_UPWIND
        weight = jnp.where(steps < 0, 0.0, pick(steps, decays))
        factors = [[weight * v for v in time[0]]]
        for d in (1, 2, 3):
            at = self.coarse(d, col)
            factors.append(
                [pick(at, [pick(steps, [z[x][i] for z in powers]) for i in range(self.pc)]) for x in range(self.p)]
            )
        return self.fine_rows(*factors)

    def face_traces(self, time, space):
        four, pc, p = self.pc**2, self.pc, self.p
        factors = [(self.over_fine(time, 0), lambda r: 0)]
        for d in (1, 2, 3):
            at = self.fine(d, iota((1, self.n), 1))
            vectors = self.over_fine(space, d)
            vectors = vectors + [(at == node).astype(F32) for node in (p - 1, 0)]

            def row_digit(r, d=d):
                face, high, low = r // four, r // pc % pc, r % pc
                if face // 2 == d - 1:
                    return pc + face % 2
                return high if d == 1 or (d == 2 and face < 2) else low

            factors.append((vectors, row_digit))
        return self.rows_of(self.nf, factors)

    def face_spread(self, space):
        col = iota((1, self.nf), 1)
        face = quotient(col, self.pc**2)
        factors = []
        for d in (1, 2, 3):
            vectors = []
            for i in range(self.pc):
                normal = jnp.where(digit(face, 1, 2) == 0, space[i][0], space[i][self.p - 1])
                tangential = (self.bit(d, face, col) == i).astype(F32)
                vectors.append(jnp.where(quotient(face, 2) == d - 1, normal, tangential))
            factors.append((vectors, functools.partial(self.coarse, d)))
        return self.rows_of(self.nc, factors)


def pieces(v):
    high = v.astype(BF16)
    return high, (v - high.astype(F32)).astype(BF16)


def bdot(a, b):
    return jnp.dot(a, b, preferred_element_type=F32)


def product(matrix, values):
    mh, ml = matrix
    vh, vl = values
    return bdot(mh, vh) + (bdot(mh, vl) + bdot(ml, vh))


def lane_select(values, indices):
    outs = []
    for j in range(0, indices.shape[-1], 128):
        at = indices[:, j : j + 128]
        tile, lane = at >> 7, at & 127
        out = jnp.zeros(at.shape, F32)
        for k in range(values.shape[-1] // 128):
            got = jnp.take_along_axis(values[:, 128 * k : 128 * k + 128], lane, axis=1, mode="promise_in_bounds")
            out = jnp.where(tile == k, got, out)
        outs.append(out)
    return jnp.concatenate(outs, axis=1)


def select_columns(values, indices, count):
    rows = values.shape[0]
    high, low = pieces(values)
    chosen = (iota((count, indices.shape[-1]), 0) == indices).astype(F32).astype(BF16)
    both = bdot(jnp.concatenate([high, low], axis=0), chosen)
    return both[:rows] + both[rows:]


def lower_half(shape):
    return iota(shape, 0) < 4


def load(ref, start, stop):
    return jnp.concatenate([ref[k, start:stop, :] for k in range(ref.shape[0])], axis=1)


def store(ref, start, values):
    for k in range(ref.shape[0]):
        ref[k, start : start + values.shape[0], :] = values[:, 128 * k : 128 * k + 128]


def accumulate(ref, start, values):
    for k in range(ref.shape[0]):
        ref[k, start : start + values.shape[0], :] += values[:, 128 * k : 128 * k + 128]


def trace_rows(ref, face, p):
    rows = ref.shape[1]
    d, node = face // 2, face % 2 * (p - 1)
    if d == 0:
        step = p * p
        parts = [load(ref, r + node * step, r + (node + 1) * step) for r in range(0, rows, p * step)]
        return jnp.concatenate(parts, axis=0)
    if d == 1:
        parts = []
        at = node * p // 8 * 8
        for r in range(0, rows, 2 * p * p):
            first = load(ref, r + at, r + at + 8)
            second = load(ref, r + p * p + at, r + p * p + at + 8)
            low = lower_half(first.shape)
            if node == 0:
                parts.append(jnp.where(low, first, pltpu.roll(second, 4, 0)))
            else:
                parts.append(jnp.where(low, pltpu.roll(first, 4, 0), second))
        return jnp.concatenate(parts, axis=0)
    parts = [ref[k, pl.ds(node, rows // p, stride=p), :] for k in range(ref.shape[0])]
    return jnp.concatenate(parts, axis=1)


def add_rows(ref, values, face, p):
    rows = ref.shape[1]
    d, node = face // 2, face % 2 * (p - 1)
    if d == 0:
        step = p * p
        for i, r in enumerate(range(0, rows, p * step)):
            accumulate(ref, r + node * step, values[i * step : (i + 1) * step])
    elif d == 1:
        at = node * p // 8 * 8
        for i, r in enumerate(range(0, rows, 2 * p * p)):
            eight = values[8 * i : 8 * i + 8]
            turned = pltpu.roll(eight, 4, 0)
            low = lower_half(eight.shape)
            if node == 0:
                first, second = jnp.where(low, eight, 0.0), jnp.where(low, turned, 0.0)
            else:
                first, second = jnp.where(low, 0.0, turned), jnp.where(low, 0.0, eight)
            accumulate(ref, r + at, first)
            accumulate(ref, r + p * p + at, second)
    else:
        for k in range(ref.shape[0]):
            where = (k, pl.ds(node, rows // p, stride=p), slice(None))
            ref[where] = ref[where] + values[:, 128 * k : 128 * k + 128]


def from_halves(ref, row):
    tiles = []
    for k in range(0, ref.shape[1], 8):
        first, second = ref[row, k : k + 8, :], ref[row + 1, k : k + 8, :]
        low = lower_half(first.shape)
        tiles.append(jnp.where(low, first, pltpu.roll(second, 4, 0)))
        tiles.append(jnp.where(low, pltpu.roll(first, 4, 0), second))
    return jnp.concatenate(tiles, axis=1)


def to_halves(ref, row, values):
    for k in range(0, ref.shape[1], 8):
        at = 32 * k
        first, second = values[:, at : at + 128], values[:, at + 128 : at + 256]
        low = lower_half(first.shape)
        ref[row, k : k + 8, :] = jnp.where(low, first, pltpu.roll(second, 4, 0))
        ref[row + 1, k : k + 8, :] = jnp.where(low, pltpu.roll(first, 4, 0), second)


def keep_pieces(ref, matrix):
    high, low = pieces(matrix)
    ref[0] = high
    ref[1] = low


def both_pieces(ref):
    return ref[0], ref[1]


def last_time(nodes):
    return (nodes.q - 1) * nodes.p**3


def is_even():
    return lax.axis_index("space") % 2 == 0


def pack(x_ref, halo_ref, first_ref, second_ref, p):
    elements = x_ref.shape[0] * 128
    to_left = select_columns(trace_rows(x_ref, 0, p), halo_ref[0:1, :], elements)
    to_right = select_columns(trace_rows(x_ref, 1, p), halo_ref[1:2, :], elements)
    even = is_even()
    first_ref[...] = jnp.where(even, to_right, to_left)
    second_ref[...] = jnp.where(even, to_left, to_right)


def sources_of(mine, peers):
    if peers & (peers - 1) == 0:
        return [mine ^ k for k in range(peers)]
    return [mine - k for k in range(peers)]


def start_kernel(
    nodes, peers, f_hbm, c_hbm, nb_hbm, halo_hbm, tb_hbm, sb_hbm, st_hbm, tr_hbm, sr_hbm, cs_hbm,
    x_ref, first_ref, second_ref, last_ref, rf_ref, c_ref, nb_ref, halo_ref,
    inverse_ref, step_ref, coarse_ref, lift_ref, spread_ref, ends_ref,
    f_ref, tb, sb, st, tr, sr, cs, small_sem, table_sem, field_sem,
):
    nodes = nodes.fresh()
    n, p, nc = nodes.n, nodes.p, nodes.nc
    rows = x_ref.shape[1]
    small = [(tb_hbm, tb), (sb_hbm, sb), (st_hbm, st), (tr_hbm, tr), (sr_hbm, sr), (cs_hbm, cs)]
    tables = [(c_hbm, c_ref), (nb_hbm, nb_ref), (halo_hbm, halo_ref)]
    small = [pltpu.make_async_copy(a, b, small_sem.at[i]) for i, (a, b) in enumerate(small)]
    tables = [pltpu.make_async_copy(a, b, table_sem.at[i]) for i, (a, b) in enumerate(tables)]
    slabs = rows // n
    size = n // p
    fields = [
        pltpu.make_async_copy(f_hbm.at[pl.ds(s * size, size)], f_ref.at[pl.ds(s * size, size)], field_sem.at[s])
        for s in range(slabs)
    ]
    for copy in small + fields + tables:
        copy.start()
    for copy in small:
        copy.wait()
    t, b, d, tt, ss, w = (scalars(ref) for ref in (tb, sb, st, tr, sr, cs))
    ti, si = two_minus(t), two_minus(b)
    et = nodes.over_fine(ti, 0)
    es = [nodes.over_fine(si, k) for k in (1, 2, 3)]
    of_b = [nodes.over_fine(b, k) for k in (1, 2, 3)]
    of_d = [nodes.over_fine(d, k) for k in (1, 2, 3)]
    of_t = nodes.over_fine(t, 0)
    inverse = pieces(nodes.fine_rows(et, *es))
    inverse_ref[0], inverse_ref[1] = inverse
    unit = (iota((n, n), 0) == iota((n, n), 1)).astype(F32)
    keep = unit - nodes.fine_rows(combine(ti, of_t), *(combine(si, v) for v in of_b))
    ed = [combine(si, v) for v in of_d]
    drift = nodes.fine_rows(et, ed[0], es[1], es[2]) + nodes.fine_rows(et, es[0], ed[1], es[2])
    drift = -(drift + nodes.fine_rows(et, es[0], es[1], ed[2]))
    keep_pieces(step_ref, jnp.concatenate([keep, drift], axis=0))
    rt = nodes.over_fine(tt, 0)
    rs = [nodes.over_fine(ss, k) for k in (1, 2, 3)]
    rd = [combine(ss, v) for v in of_d]
    block = nodes.coarse_rows(combine(tt, of_t), *(combine(ss, v) for v in of_b))
    stiff = nodes.coarse_rows(rt, rd[0], rs[1], rs[2]) + nodes.coarse_rows(rt, rs[0], rd[1], rs[2])
    stiff = stiff + nodes.coarse_rows(rt, rs[0], rs[1], rd[2])
    restrict = nodes.coarse_rows(rt, *rs)
    keep_pieces(coarse_ref, jnp.concatenate([restrict, block, stiff, nodes.face_traces(tt, ss)], axis=0))
    mine = lax.axis_index("slab")
    keep_pieces(lift_ref, nodes.lifted(tt, ss, w, mine, sources_of(mine, peers)))
    spread_ref[...] = nodes.face_spread(ss)
    sub = iota((8, 128), 0)
    half = nodes.pc**2
    ends_ref[0] = jnp.where(sub < half, ss[0][0], ss[1][0])
    ends_ref[1] = jnp.where(sub < half, ss[0][p - 1], ss[1][p - 1])
    tables[0].wait()
    scale = 1.0 / c_ref[...]
    total = 0.0
    for s in range(slabs):
        fields[s].wait()
        f = jnp.concatenate([from_halves(f_ref, (s * n + r) // p) for r in range(0, n, 8)], axis=0)
        total = total + f
        store(x_ref, s * n, product(inverse, pieces(f)) * scale)
    tables[1].wait()
    tables[2].wait()
    pack(x_ref, halo_ref, first_ref, second_ref, p)
    last_ref[...] = load(x_ref, rows - n + last_time(nodes), rows)
    high, low = pieces(restrict)
    rf_ref[...] = product((high, low), pieces(total))


def local_kernel(nodes, x_ref, x1_ref, c_ref, nb_ref, step_ref, base_ref, g_ref):
    n, p = nodes.n, nodes.p
    rows = x_ref.shape[1]
    elements = x_ref.shape[0] * 128
    c = c_ref[...]
    scale = 1.0 / c
    g_ref[...] = jnp.zeros_like(g_ref)
    for s in range(1, rows // n):
        before = (s - 1) * n + last_time(nodes)
        store(g_ref, s * n, UPWIND * c * load(x_ref, before, before + p**3))
    step = both_pieces(step_ref)
    for face in range(6):
        values = trace_rows(x_ref, face ^ 1, p)
        add_rows(g_ref, PENALTY * select_columns(values, nb_ref[face : face + 1, :], elements), face, p)
    for s in range(rows // n):
        moved = product(step, pieces(load(x_ref, s * n, (s + 1) * n)))
        store(base_ref, s * n, load(x1_ref, s * n, (s + 1) * n) + moved[:n] + scale * moved[n:])


def finish(nodes, base_ref, g_ref, got_first, got_second, prev_a, prev_b, c_ref, nb_ref, inverse_ref, x_ref):
    n, p = nodes.n, nodes.p
    rows = base_ref.shape[1]
    elements = base_ref.shape[0] * 128
    inverse = both_pieces(inverse_ref)
    c = c_ref[...]
    scale = 1.0 / c
    even = is_even()
    first, second = got_first[...], got_second[...]
    left, right = jnp.where(even, second, first), jnp.where(even, first, second)
    count = left.shape[-1]
    left = PENALTY * select_columns(left, nb_ref[0:1, :] - elements, count)
    right = PENALTY * select_columns(right, nb_ref[1:2, :] - (elements + count), count)
    handed = (UPWIND * c) * (prev_a[...] + prev_b[...])
    step = p * p
    for s in range(rows // n):
        parts = []
        for time in range(nodes.q):
            at = (s * nodes.q + time) * step
            for x in range(p):
                start = s * n + time * p**3 + x * step
                part = load(g_ref, start, start + step)
                if x == 0:
                    part = part + left[at : at + step]
                if x == p - 1:
                    part = part + right[at : at + step]
                if s == 0 and time == 0:
                    part = part + handed[x * step : (x + 1) * step]
                parts.append(part)
        moved = product(inverse, pieces(jnp.concatenate(parts, axis=0)))
        store(x_ref, s * n, load(base_ref, s * n, (s + 1) * n) + scale * moved)


def finish_kernel(
    nodes, base_ref, g_ref, got_first, got_second, prev_a, prev_b, c_ref, nb_ref, inverse_ref, halo_ref,
    x_ref, first_ref, second_ref, last_ref,
):
    finish(nodes, base_ref, g_ref, got_first, got_second, prev_a, prev_b, c_ref, nb_ref, inverse_ref, x_ref)
    rows = base_ref.shape[1]
    pack(x_ref, halo_ref, first_ref, second_ref, nodes.p)
    last_ref[...] = load(x_ref, rows - nodes.n + last_time(nodes), rows)


def coarse_kernel(
    nodes, base_ref, g_ref, got_first, got_second, prev_a, prev_b, c_ref, nb_ref, inverse_ref, halo_ref,
    coarse_ref, spread_ref, rf_ref,
    x_ref, packed_ref, local_ref,
):
    finish(nodes, base_ref, g_ref, got_first, got_second, prev_a, prev_b, c_ref, nb_ref, inverse_ref, x_ref)
    n, p, nc = nodes.n, nodes.p, nodes.nc
    rows = x_ref.shape[1]
    elements = x_ref.shape[0] * 128
    half = nodes.pc**2
    high, low = both_pieces(coarse_ref)
    total = load(x_ref, 0, n)
    before = 0.0
    for k in range(1, rows // n):
        total = total + load(x_ref, k * n, (k + 1) * n)
        at = (k - 1) * n + last_time(nodes)
        before = before + load(x_ref, at, at + p**3)
    applied = product((high, low), pieces(total))[nc:]
    traces = applied[2 * nc :]
    halo = halo_ref[...]
    packed_ref[...] = lane_select(
        traces[:8], jnp.where(iota((8, halo.shape[-1]), 0) < half, halo[1:2, :], halo[0:1, :])
    )
    low_half = iota((8, elements), 0) < half
    coupled = [
        lane_select(
            traces[8 * k : 8 * k + 8],
            jnp.where(low_half, nb_ref[2 * k : 2 * k + 1, :], nb_ref[2 * k + 1 : 2 * k + 2, :]),
        )
        for k in range(3)
    ]
    c = c_ref[...]
    end = load(x_ref, rows - n + last_time(nodes), rows)
    plane = p**3
    moved = product((high[:, :plane], low[:, :plane]), pieces(jnp.concatenate([before, end], axis=1)))[:nc]
    local = rf_ref[...] - c * applied[:nc] - applied[nc : 2 * nc] + (UPWIND * c) * moved[:, :elements]
    spread = product(pieces(spread_ref[...]), pieces(jnp.concatenate(coupled, axis=0)))
    local_ref[:nc, :] = local + PENALTY * spread
    local_ref[nc:, :] = UPWIND * moved[:, elements:]


def group_kernel(nodes, local_ref, got_first, got_second, c_ref, nb_ref, ends_ref, out_ref):
    nc = nodes.nc
    elements = local_ref.shape[-1]
    half = nodes.pc**2
    first, second = got_first[...], got_second[...]
    count = first.shape[-1]
    even = is_even()
    left, right = jnp.where(even, second, first), jnp.where(even, first, second)
    both = jnp.where(iota((8, count), 0) < half, left, right)
    low = iota((8, elements), 0) < half
    at = jnp.where(low, nb_ref[0:1, :] - elements, nb_ref[1:2, :] - (elements + count))
    got = lane_select(both, at)
    turned = pltpu.roll(got, half, 0)
    from_left, from_right = jnp.where(low, got, turned), jnp.where(low, turned, got)
    tiles = elements // 128
    a, b = jnp.concatenate([ends_ref[0]] * tiles, axis=1), jnp.concatenate([ends_ref[1]] * tiles, axis=1)
    total = local_ref[:nc, :] + PENALTY * (a * from_left + b * from_right)
    out_ref[:nc, :] = total / c_ref[...]
    out_ref[nc:, :] = local_ref[nc:, :]


def end_kernel(nodes, x_ref, lift_ref, *refs):
    parts, (out_hbm, out_ref, sem) = refs[:-3], refs[-3:]
    n, p = nodes.n, nodes.p
    every = jnp.concatenate([ref[...] for ref in parts], axis=0)
    lifted = product(both_pieces(lift_ref), pieces(every))
    rows = x_ref.shape[1]
    size = n // p
    copies = []
    for s in range(rows // n):
        for r in range(0, n, 8):
            at = s * n + r
            to_halves(out_ref, at // p, load(x_ref, at, at + 8) + lifted[r : r + 8, :])
        here = pl.ds(s * size, size)
        copies.append(pltpu.make_async_copy(out_ref.at[here], out_hbm.at[here], sem.at[s]))
        copies[-1].start()
    for copy in copies:
        copy.wait()


def call(kernel, args, outs, scratch=(), hbm_in=False, hbm_out=False):
    spaces = [pltpu.HBM if flag else pltpu.VMEM for flag in (hbm_in, hbm_out)]
    return pl.pallas_call(
        kernel,
        out_shape=[jax.ShapeDtypeStruct(shape, dtype) for shape, dtype in outs],
        in_specs=[pl.BlockSpec(memory_space=spaces[0])] * len(args),
        out_specs=[pl.BlockSpec(memory_space=spaces[1])] * len(outs),
        scratch_shapes=scratch,
        compiler_params=pltpu.CompilerParams(vmem_limit_bytes=VMEM_BYTES),
        name=kernel.func.__name__,
    )(*args)


def swapped(first, second):
    peers = lax.axis_size("space")
    pairs = [[], []]
    for i in range(peers - 1):
        pairs[i % 2] += [(i, i + 1), (i + 1, i)]
    return [lax.ppermute(v, "space", q) for v, q in zip((first, second), pairs)]


def handed_on(last):
    peers = lax.axis_size("slab")
    return [lax.ppermute(last, "slab", [(i, i + 1) for i in range(k, peers - 1, 2)]) for k in (0, 1)]


def earlier(mine):
    peers = lax.axis_size("slab")
    parts = [mine]
    for k in range(1, peers):
        pairs = [(sources_of(i, peers)[k], i) for i in range(peers)]
        parts.append(lax.ppermute(mine, "slab", [(a, b) for a, b in pairs if 0 <= a < b]))
    return parts


def body(
    forcing, coefficient, neighbours, halo_faces, time_block, space_block, stiffness, time_restrict, space_restrict,
    coarse_smoother,
):
    slabs, q, p = forcing.shape[:3]
    elements = forcing.shape[-1]
    peers = lax.axis_size("slab")
    nodes = Nodes(q, p, space_restrict.shape[0])
    n, nc = nodes.n, nodes.nc
    rows = slabs * n
    count = halo_faces.shape[-1]
    tiles = elements // 128
    halves = (rows // p, tiles * p, 128)
    f = forcing.reshape(rows // p, p, tiles, 128).transpose(0, 2, 1, 3).reshape(halves)
    field = ((tiles, rows, 128), F32)
    face = ((rows // p, count), F32)
    plane = ((p**3, elements), F32)
    small = (time_block, space_block, stiffness, time_restrict, space_restrict, coarse_smoother)
    (
        x1, first, second, last, rf, c, nb, halo, inverse, step, coarse, lift, spread, ends
    ) = call(
        functools.partial(start_kernel, nodes, peers),
        (f, coefficient.reshape(1, elements), neighbours, halo_faces) + small,
        (
            field, face, face, plane, ((nc, elements), F32), ((1, elements), F32), (neighbours.shape, jnp.int32),
            (halo_faces.shape, jnp.int32), ((2, n, n), BF16), ((2, 2 * n, n), BF16), ((2, 3 * nc + nodes.nf, n), BF16),
            ((2, n, 2 * nc * peers), BF16), ((nc, nodes.nf), F32), ((2, 8, 128), F32),
        ),
        [pltpu.VMEM(halves, F32)]
        + [pltpu.SMEM(v.shape, F32) for v in small]
        + [pltpu.SemaphoreType.DMA((len(small),)), pltpu.SemaphoreType.DMA((3,)), pltpu.SemaphoreType.DMA((slabs,))],
        hbm_in=True,
    )
    x = x1
    for sweep in range(SWEEPS - 1):
        got = swapped(first, second) + handed_on(last)
        base, g = call(functools.partial(local_kernel, nodes), (x, x1, c, nb, step), (field, field))
        args = (base, g, *got, c, nb, inverse, halo)
        if sweep < SWEEPS - 2:
            x, first, second, last = call(functools.partial(finish_kernel, nodes), args, (field, face, face, plane))
        else:
            x, packed, local = call(
                functools.partial(coarse_kernel, nodes), args + (coarse, spread, rf),
                (field, ((8, count), F32), ((2 * nc, elements), F32)),
            )
    got = swapped(packed, packed)
    (mine,) = call(
        functools.partial(group_kernel, nodes), (local, *got, c, nb, ends), (((2 * nc, elements), F32),)
    )
    (out,) = call(
        functools.partial(end_kernel, nodes), (x, lift, *earlier(mine)), ((halves, F32),),
        [pltpu.VMEM(halves, F32), pltpu.SemaphoreType.DMA((slabs,))], hbm_out=True,
    )
    out = out.reshape(rows // p, tiles, p, 128).transpose(0, 2, 1, 3)
    return out.reshape(forcing.shape)


def solution(mesh):
    in_specs = (
        P("slab", None, None, None, None, "space"),
        P("space"),
        P(None, "space"),
        P(None, "space"),
        P(),
        P(),
        P(),
        P(),
        P(),
        P(),
    )
    out_specs = P("slab", None, None, None, None, "space")
    return jax.shard_map(body, mesh=mesh, in_specs=in_specs, out_specs=out_specs, check_vma=False)
```

time: 65.5 us -> 59.6 us (0.910); the launches traced: 65.1 us -> 58.5 us
  blocking collectives: 8.74 us -> 0 us
  Pallas kernels: 26.8 us -> 18.8 us
  starting transfers between devices: 20.4 us -> 25.7 us
  waiting for transfers between devices: 3.46 us -> 6.08 us
  local copies, waits for them, and re-layouts: 5.52 us -> 7.59 us
    all_gather x1 -> x0, blocking collectives: 8.74 us -> none  [body(): every = lax.all_gather(mine, 'slab', axis=0, tiled=True)]
    pallas_call x7, Pallas kernels: 26.8 us -> 18.8 us  [call(): pl.pallas_call(kernel, out_shape=[jax.ShapeDtypeStruct(shape, dtype) for...]
    ppermute x0 -> x3, starting transfers between devices: none -> 5.86 us  [earlier(): lax.ppermute(mine, 'slab', [(a, b) for a, b in pairs if 0 <= a < b])]
    ppermute x0 -> x3, waiting for transfers between devices: none -> 2.38 us  [earlier(): lax.ppermute(mine, 'slab', [(a, b) for a, b in pairs if 0 <= a < b])]
    unnamed x30 -> x20, local copies, waits for them, and re-layouts: 5.52 us -> 7.59 us
    ppermute x6, starting transfers between devices: 12.1 us -> 11.2 us  [swapped(): return [lax.ppermute(v, 'space', q) for v, q in zip((first, second), pairs)]]
  transfers between devices with their start and end apart: 10 -> 13, of which waited for: 1 -> 5; matrix products, arithmetic and copies ran while one was open for 0% -> 0% of each run, Pallas kernels for 19% -> 16%
where the time goes in v2:
time: 59.6 us; the launch traced here: 58.5 us
  starting transfers between devices  25.7 us (43%)
  Pallas kernels  18.8 us (32%)
  local copies, waits for them, and re-layouts  7.59 us (13%)
  waiting for transfers between devices  6.08 us (10%)
    pallas_call x7, Pallas kernels, call(): pl.pallas_call(kernel, out_shape=[jax.ShapeDtypeStruct(shape, dtype) for...  18.8 us
    ppermute x6, starting transfers between devices, swapped(): return [lax.ppermute(v, 'space', q) for v, q in zip((first, second), pairs)]  11.2 us
    ppermute x4, starting transfers between devices, handed_on(): lax.ppermute(last, 'slab', [(i, i + 1) for i in range(k, peers - 1, 2)])  8.67 us
    unnamed x20, local copies, waits for them, and re-layouts  7.59 us
    ppermute x3, starting transfers between devices, earlier(): lax.ppermute(mine, 'slab', [(a, b) for a, b in pairs if 0 <= a < b])  5.86 us
    ppermute x6, waiting for transfers between devices, swapped(): return [lax.ppermute(v, 'space', q) for v, q in zip((first, second), pairs)]  3.68 us
    ppermute x3, waiting for transfers between devices, earlier(): lax.ppermute(mine, 'slab', [(a, b) for a, b in pairs if 0 <= a < b])  2.38 us
  transfers between devices with their start and end apart: 13, of which 5 were waited for; matrix products, arithmetic and copies ran while one was open for 0% of the time, Pallas kernels for 16%

profile of v2, /device:TPU:9, one launch (start us, length us, event | category | flops | bytes accessed | tf_op | source)
XLA Modules:
  0.0 58.5 jit_solution(8707438451387897445)
XLA Ops:
  0.0 1.4 %copy-done = f32[2,3,4,4,4,1024]{5,4,3,2,1,0:T(4,128)S(1)} copy-done((f32[2,3,4,4,4,1024]{5,4,3,2,1,0:T(4,128)S(1)}, f32[2,3,4,4,4,1024]{5,4,3,2,1,0:T(4,128)}, u32[]{:S(2)}) %copy-start) | copy-done | bytes 1572888
  7.6 2.9 %start_kernel.1 = (f32[8,384,128]{2,1,0:T(8,128)S(1)}, f32[96,512]{1,0:T(8,128)S(1)}, f32[96,512]{1,0:T(8,128)S(1)}, f32[64,1024]{1,0:T(8,128)S(1)}, f32[8,1024]...) custom-call(f32[96,32,128]{2,1,0:T(8,128)S(1)} %bitcast.11, ...), custom_call_target="tpu_custom_call" | custom-call | tf_op jit(solution)/shard_map/start_kernel/pallas_call | solution.py:559
  10.5 3.7 %collective-permute-start.3 = (f32[64,1024]{1,0:T(8,128)S(1)}, f32[64,1024]{1,0:T(8,128)S(1)}, u32[]{:S(2)}, u32[]{:S(2)}) collective-permute-start(f32[64,1024]{1,0:T(8,128)S(1)} %get-tuple-element.38), channel_id=1, source_target_pairs={{8,16},{9,17},{10,18},{11,19},{12,20},{13,21},{14,22},{15,23}} | collective-permute-start | bytes 786440 | tf_op jit(solution)/shard_map/ppermute | solution.py:580
  14.2 1.3 %collective-permute-start.2 = (f32[64,1024]{1,0:T(8,128)S(1)}, f32[64,1024]{1,0:T(8,128)S(1)}, u32[]{:S(2)}, u32[]{:S(2)}) collective-permute-start(f32[64,1024]{1,0:T(8,128)S(1)} %get-tuple-element.38), channel_id=1, source_target_pairs={{0,8},{16,24},{1,9},{17,25},{2,10},{18,26},{3,11},{19,27},{4,12},{... | collective-permute-start | bytes 786440 | tf_op jit(solution)/shard_map/ppermute | solution.py:580
  15.5 1.3 %collective-permute-start = (f32[96,512]{1,0:T(8,128)S(1)}, f32[96,512]{1,0:T(8,128)S(1)}, u32[]{:S(2)}, u32[]{:S(2)}) collective-permute-start(f32[96,512]{1,0:T(8,128)S(1)} %get-tuple-element.36), channel_id=1, source_target_pairs={{0,1},{1,0},{2,3},{3,2},{4,5},{5,4},{6,7},{7,6},{8,9},{9,8},{10,11... | collective-permute-start | bytes 589832 | tf_op jit(solution)/shard_map/ppermute | solution.py:575
  16.8 2.0 %collective-permute-start.1 = (f32[96,512]{1,0:T(8,128)S(1)}, f32[96,512]{1,0:T(8,128)S(1)}, u32[]{:S(2)}, u32[]{:S(2)}) collective-permute-start(f32[96,512]{1,0:T(8,128)S(1)} %get-tuple-element.37), channel_id=1, source_target_pairs={{1,2},{2,1},{3,4},{4,3},{5,6},{6,5},{9,10},{10,9},{11,12},{12,11},... | collective-permute-start | bytes 589832 | tf_op jit(solution)/shard_map/ppermute | solution.py:575
  18.9 4.7 %local_kernel.2 = (f32[8,384,128]{2,1,0:T(8,128)S(1)}, f32[8,384,128]{2,1,0:T(8,128)S(1)}) custom-call(f32[8,384,128]{2,1,0:T(8,128)S(1)} %get-tuple-element.30.x_ref.x1_ref, f32[8,384,128]{2,1,0:T(8,128)S(1)} %get-tuple-element.30.x_ref.x1_ref, f32[1,1024]{1,0:T(1,128)S(1)} %get-tuple-element.31.c_ref, s32[6,1024]{1,0:T(8,128)S(1)} %get-tuple-element.32.nb_ref, ...), custom_call_target="tpu_custom_call" | custom-call | tf_op jit(solution)/shard_map/local_kernel/pallas_call | solution.py:559
  23.6 1.2 %collective-permute-done.1.got_second = f32[96,512]{1,0:T(8,128)S(1)} collective-permute-done((f32[96,512]{1,0:T(8,128)S(1)}, f32[96,512]{1,0:T(8,128)S(1)}, u32[]{:S(2)}, u32[]{:S(2)}) %collective-permute-start.1) | collective-permute-done | bytes 196640 | tf_op jit(solution)/shard_map/ppermute | solution.py:575
  24.8 2.1 %finish_kernel.1 = (f32[8,384,128]{2,1,0:T(8,128)S(1)}, f32[96,512]{1,0:T(8,128)S(1)}, f32[96,512]{1,0:T(8,128)S(1)}, f32[64,1024]{1,0:T(8,128)S(1)}) custom-call(f32[8,384,128]{2,1,0:T(8,128)S(1)} %get-tuple-element.34.base_ref, f32[8,384,128]{2,1,0:T(8,128)S(1)} %get-tuple-element.35.g_ref, f32[96,512]{1,0:T(8,128)S(1)} %collective-permute-done.got_first, ...), custom_call_target="tpu_custom_call" | custom-call | tf_op jit(solution)/shard_map/finish_kernel/pallas_call | solution.py:559
  26.9 2.4 %collective-permute-start.7 = (f32[64,1024]{1,0:T(8,128)S(1)}, f32[64,1024]{1,0:T(8,128)S(1)}, u32[]{:S(2)}, u32[]{:S(2)}) collective-permute-start(f32[64,1024]{1,0:T(8,128)S(1)} %get-tuple-element.46), channel_id=1, source_target_pairs={{8,16},{9,17},{10,18},{11,19},{12,20},{13,21},{14,22},{15,23}} | collective-permute-start | bytes 786440 | tf_op jit(solution)/shard_map/ppermute | solution.py:580
  29.3 1.3 %collective-permute-start.6 = (f32[64,1024]{1,0:T(8,128)S(1)}, f32[64,1024]{1,0:T(8,128)S(1)}, u32[]{:S(2)}, u32[]{:S(2)}) collective-permute-start(f32[64,1024]{1,0:T(8,128)S(1)} %get-tuple-element.46), channel_id=1, source_target_pairs={{0,8},{16,24},{1,9},{17,25},{2,10},{18,26},{3,11},{19,27},{4,12},{... | collective-permute-start | bytes 786440 | tf_op jit(solution)/shard_map/ppermute | solution.py:580
  30.6 1.3 %collective-permute-start.4 = (f32[96,512]{1,0:T(8,128)S(1)}, f32[96,512]{1,0:T(8,128)S(1)}, u32[]{:S(2)}, u32[]{:S(2)}) collective-permute-start(f32[96,512]{1,0:T(8,128)S(1)} %get-tuple-element.44), channel_id=1, source_target_pairs={{0,1},{1,0},{2,3},{3,2},{4,5},{5,4},{6,7},{7,6},{8,9},{9,8},{10,11... | collective-permute-start | bytes 589832 | tf_op jit(solution)/shard_map/ppermute | solution.py:575
  31.9 2.1 %collective-permute-start.5 = (f32[96,512]{1,0:T(8,128)S(1)}, f32[96,512]{1,0:T(8,128)S(1)}, u32[]{:S(2)}, u32[]{:S(2)}) collective-permute-start(f32[96,512]{1,0:T(8,128)S(1)} %get-tuple-element.45), channel_id=1, source_target_pairs={{1,2},{2,1},{3,4},{4,3},{5,6},{6,5},{9,10},{10,9},{11,12},{12,11},... | collective-permute-start | bytes 589832 | tf_op jit(solution)/shard_map/ppermute | solution.py:575
  34.0 4.7 %local_kernel.3 = (f32[8,384,128]{2,1,0:T(8,128)S(1)}, f32[8,384,128]{2,1,0:T(8,128)S(1)}) custom-call(f32[8,384,128]{2,1,0:T(8,128)S(1)} %get-tuple-element.41.x_ref, f32[8,384,128]{2,1,0:T(8,128)S(1)} %get-tuple-element.30.x_ref.x1_ref, f32[1,1024]{1,0:T(1,128)S(1)} %get-tuple-element.31.c_ref, s32[6,1024]{1,0:T(8,128)S(1)} %get-tuple-element.32.nb_ref, ...), custom_call_target="tpu_custom_call" | custom-call | tf_op jit(solution)/shard_map/local_kernel/pallas_call | solution.py:559
  38.7 1.1 %collective-permute-done.5.got_second = f32[96,512]{1,0:T(8,128)S(1)} collective-permute-done((f32[96,512]{1,0:T(8,128)S(1)}, f32[96,512]{1,0:T(8,128)S(1)}, u32[]{:S(2)}, u32[]{:S(2)}) %collective-permute-start.5) | collective-permute-done | bytes 196640 | tf_op jit(solution)/shard_map/ppermute | solution.py:575
  39.8 2.5 %coarse_kernel.1 = (f32[8,384,128]{2,1,0:T(8,128)S(1)}, f32[8,512]{1,0:T(8,128)S(1)}, f32[16,1024]{1,0:T(8,128)S(1)}) custom-call(f32[8,384,128]{2,1,0:T(8,128)S(1)} %get-tuple-element.42.base_ref, f32[8,384,128]{2,1,0:T(8,128)S(1)} %get-tuple-element.43.g_ref, f32[96,512]{1,0:T(8,128)S(1)} %collective-permute-done.4.got_first, ...), custom_call_target="tpu_custom_call" | custom-call | tf_op jit(solution)/shard_map/coarse_kernel/pallas_call | solution.py:559
  42.3 3.2 %collective-permute-start.9 = (f32[8,512]{1,0:T(8,128)S(1)}, f32[8,512]{1,0:T(8,128)S(1)}, u32[]{:S(2)}, u32[]{:S(2)}) collective-permute-start(f32[8,512]{1,0:T(8,128)S(1)} %get-tuple-element.53), channel_id=1, source_target_pairs={{1,2},{2,1},{3,4},{4,3},{5,6},{6,5},{9,10},{10,9},{11,12},{12,11},... | collective-permute-start | bytes 49160 | tf_op jit(solution)/shard_map/ppermute | solution.py:575
  45.5 1.3 %collective-permute-start.8 = (f32[8,512]{1,0:T(8,128)S(1)}, f32[8,512]{1,0:T(8,128)S(1)}, u32[]{:S(2)}, u32[]{:S(2)}) collective-permute-start(f32[8,512]{1,0:T(8,128)S(1)} %get-tuple-element.53), channel_id=1, source_target_pairs={{0,1},{1,0},{2,3},{3,2},{4,5},{5,4},{6,7},{7,6},{8,9},{9,8},{10,11... | collective-permute-start | bytes 49160 | tf_op jit(solution)/shard_map/ppermute | solution.py:575
  46.8 0.9 %collective-permute-done.9.got_second = f32[8,512]{1,0:T(8,128)S(1)} collective-permute-done((f32[8,512]{1,0:T(8,128)S(1)}, f32[8,512]{1,0:T(8,128)S(1)}, u32[]{:S(2)}, u32[]{:S(2)}) %collective-permute-start.9) | collective-permute-done | bytes 16416 | tf_op jit(solution)/shard_map/ppermute | solution.py:575
  48.4 3.3 %collective-permute-start.12 = (f32[16,1024]{1,0:T(8,128)S(1)}, f32[16,1024]{1,0:T(8,128)S(1)}, u32[]{:S(2)}, u32[]{:S(2)}) collective-permute-start(f32[16,1024]{1,0:T(8,128)S(1)} %group_kernel.1.refs_0_), channel_id=1, source_target_pairs={{8,16},{0,24},{9,17},{1,25},{10,18},{2,26},{11,19},{3,27},{12,20},... | collective-permute-start | bytes 196616 | tf_op jit(solution)/shard_map/ppermute | solution.py:588
  51.6 1.3 %collective-permute-start.11 = (f32[16,1024]{1,0:T(8,128)S(1)}, f32[16,1024]{1,0:T(8,128)S(1)}, u32[]{:S(2)}, u32[]{:S(2)}) collective-permute-start(f32[16,1024]{1,0:T(8,128)S(1)} %group_kernel.1.refs_0_), channel_id=1, source_target_pairs={{0,16},{8,24},{1,17},{9,25},{2,18},{10,26},{3,19},{11,27},{4,20},{... | collective-permute-start | bytes 196616 | tf_op jit(solution)/shard_map/ppermute | solution.py:588
  52.9 1.3 %collective-permute-start.10 = (f32[16,1024]{1,0:T(8,128)S(1)}, f32[16,1024]{1,0:T(8,128)S(1)}, u32[]{:S(2)}, u32[]{:S(2)}) collective-permute-start(f32[16,1024]{1,0:T(8,128)S(1)} %group_kernel.1.refs_0_), channel_id=1, source_target_pairs={{0,8},{16,24},{1,9},{17,25},{2,10},{18,26},{3,11},{19,27},{4,12},{... | collective-permute-start | bytes 196616 | tf_op jit(solution)/shard_map/ppermute | solution.py:588
  54.3 2.4 %collective-permute-done.10.refs_1_ = f32[16,1024]{1,0:T(8,128)S(1)} collective-permute-done((f32[16,1024]{1,0:T(8,128)S(1)}, f32[16,1024]{1,0:T(8,128)S(1)}, u32[]{:S(2)}, u32[]{:S(2)}) %collective-permute-start.10) | collective-permute-done | bytes 65568 | tf_op jit(solution)/shard_map/ppermute | solution.py:588
  56.6 1.7 %end_kernel.1 = f32[96,32,128]{2,1,0:T(8,128)} custom-call(f32[8,384,128]{2,1,0:T(8,128)S(1)} %get-tuple-element.50.x_ref, bf16[2,192,64]{2,1,0:T(8,128)(2,1)S(1)} %get-tuple-element.51.lift_ref, f32[16,1024]{1,0:T(8,128)S(1)} %group_kernel.1.refs_0_, f32[16,1024]{1,0:T(8,128)S(1)} %collective-permute-done.10.refs_1_, ...), custom_call_target="tpu_custom_call" | custom-call | tf_op jit(solution)/shard_map/end_kernel/pallas_call | solution.py:559
  (29 shorter events, 6.8 us)
Async XLA Ops:
  0.0 1.4 %copy-start = (f32[2,3,4,4,4,1024]{5,4,3,2,1,0:T(4,128)S(1)}, f32[2,3,4,4,4,1024]{5,4,3,2,1,0:T(4,128)}, u32[]{:S(2)}) copy-start(f32[2,3,4,4,4,1024]{5,4,3,2,1,0:T(4,128)} %param.10) | copy-start | bytes 4718596
  1.4 0.8 %copy-start.1 = (s32[6,1024]{1,0:T(8,128)S(1)}, s32[6,1024]{1,0:T(8,128)}, u32[]{:S(2)}) copy-start(s32[6,1024]{1,0:T(8,128)} %nb_hbm.1) | copy-start | bytes 73732
  2.2 0.7 %copy-start.2 = (f32[1024]{0:T(1024)S(1)}, f32[1024]{0:T(1024)}, u32[]{:S(2)}) copy-start(f32[1024]{0:T(1024)} %param.11) | copy-start | bytes 12292
  2.9 0.7 %copy-start.3 = (s32[2,512]{1,0:T(2,128)S(1)}, s32[2,512]{1,0:T(2,128)}, u32[]{:S(2)}) copy-start(s32[2,512]{1,0:T(2,128)} %halo_hbm.1) | copy-start | bytes 12292
  3.5 0.7 %copy-start.4 = (f32[3,3]{1,0:T(4,128)S(1)}, f32[3,3]{1,0:T(4,128)}, u32[]{:S(2)}) copy-start(f32[3,3]{1,0:T(4,128)} %tb_hbm.1) | copy-start | bytes 112
  4.2 0.7 %copy-start.5 = (f32[4,4]{1,0:T(4,128)S(1)}, f32[4,4]{1,0:T(4,128)}, u32[]{:S(2)}) copy-start(f32[4,4]{1,0:T(4,128)} %sb_hbm.1) | copy-start | bytes 196
  4.9 0.7 %copy-start.6 = (f32[4,4]{1,0:T(4,128)S(1)}, f32[4,4]{1,0:T(4,128)}, u32[]{:S(2)}) copy-start(f32[4,4]{1,0:T(4,128)} %st_hbm.1) | copy-start | bytes 196
  5.6 0.7 %copy-start.7 = (f32[2,4]{1,0:T(2,128)S(1)}, f32[2,4]{1,0:T(2,128)}, u32[]{:S(2)}) copy-start(f32[2,4]{1,0:T(2,128)} %sr_hbm.1) | copy-start | bytes 100
  6.3 0.7 %copy-start.8 = (f32[2,2]{1,0:T(2,128)S(1)}, f32[2,2]{1,0:T(2,128)}, u32[]{:S(2)}) copy-start(f32[2,2]{1,0:T(2,128)} %cs_hbm.1) | copy-start | bytes 52
  6.9 0.7 %copy-start.9 = (f32[1,3]{1,0:T(1,128)S(1)}, f32[1,3]{1,0:T(1,128)}, u32[]{:S(2)}) copy-start(f32[1,3]{1,0:T(1,128)} %tr_hbm.1) | copy-start | bytes 40
  10.5 14.2 %collective-permute-start.3 = (f32[64,1024]{1,0:T(8,128)S(1)}, f32[64,1024]{1,0:T(8,128)S(1)}, u32[]{:S(2)}, u32[]{:S(2)}) collective-permute-start(f32[64,1024]{1,0:T(8,128)S(1)} %get-tuple-element.38), channel_id=1, source_target_pairs={{8,16},{9,17},{10,18},{11,19},{12,20},{13,21},{14,22},{15,23}} | collective-permute-start | bytes 786440 | tf_op jit(solution)/shard_map/ppermute | solution.py:580
  14.2 10.5 %collective-permute-start.2 = (f32[64,1024]{1,0:T(8,128)S(1)}, f32[64,1024]{1,0:T(8,128)S(1)}, u32[]{:S(2)}, u32[]{:S(2)}) collective-permute-start(f32[64,1024]{1,0:T(8,128)S(1)} %get-tuple-element.38), channel_id=1, source_target_pairs={{0,8},{16,24},{1,9},{17,25},{2,10},{18,26},{3,11},{19,27},{4,12},{... | collective-permute-start | bytes 786440 | tf_op jit(solution)/shard_map/ppermute | solution.py:580
  15.5 8.0 %collective-permute-start = (f32[96,512]{1,0:T(8,128)S(1)}, f32[96,512]{1,0:T(8,128)S(1)}, u32[]{:S(2)}, u32[]{:S(2)}) collective-permute-start(f32[96,512]{1,0:T(8,128)S(1)} %get-tuple-element.36), channel_id=1, source_target_pairs={{0,1},{1,0},{2,3},{3,2},{4,5},{5,4},{6,7},{7,6},{8,9},{9,8},{10,11... | collective-permute-start | bytes 589832 | tf_op jit(solution)/shard_map/ppermute | solution.py:575
  16.8 7.9 %collective-permute-start.1 = (f32[96,512]{1,0:T(8,128)S(1)}, f32[96,512]{1,0:T(8,128)S(1)}, u32[]{:S(2)}, u32[]{:S(2)}) collective-permute-start(f32[96,512]{1,0:T(8,128)S(1)} %get-tuple-element.37), channel_id=1, source_target_pairs={{1,2},{2,1},{3,4},{4,3},{5,6},{6,5},{9,10},{10,9},{11,12},{12,11},... | collective-permute-start | bytes 589832 | tf_op jit(solution)/shard_map/ppermute | solution.py:575
  26.9 12.9 %collective-permute-start.7 = (f32[64,1024]{1,0:T(8,128)S(1)}, f32[64,1024]{1,0:T(8,128)S(1)}, u32[]{:S(2)}, u32[]{:S(2)}) collective-permute-start(f32[64,1024]{1,0:T(8,128)S(1)} %get-tuple-element.46), channel_id=1, source_target_pairs={{8,16},{9,17},{10,18},{11,19},{12,20},{13,21},{14,22},{15,23}} | collective-permute-start | bytes 786440 | tf_op jit(solution)/shard_map/ppermute | solution.py:580
  29.3 10.5 %collective-permute-start.6 = (f32[64,1024]{1,0:T(8,128)S(1)}, f32[64,1024]{1,0:T(8,128)S(1)}, u32[]{:S(2)}, u32[]{:S(2)}) collective-permute-start(f32[64,1024]{1,0:T(8,128)S(1)} %get-tuple-element.46), channel_id=1, source_target_pairs={{0,8},{16,24},{1,9},{17,25},{2,10},{18,26},{3,11},{19,27},{4,12},{... | collective-permute-start | bytes 786440 | tf_op jit(solution)/shard_map/ppermute | solution.py:580
  30.6 8.1 %collective-permute-start.4 = (f32[96,512]{1,0:T(8,128)S(1)}, f32[96,512]{1,0:T(8,128)S(1)}, u32[]{:S(2)}, u32[]{:S(2)}) collective-permute-start(f32[96,512]{1,0:T(8,128)S(1)} %get-tuple-element.44), channel_id=1, source_target_pairs={{0,1},{1,0},{2,3},{3,2},{4,5},{5,4},{6,7},{7,6},{8,9},{9,8},{10,11... | collective-permute-start | bytes 589832 | tf_op jit(solution)/shard_map/ppermute | solution.py:575
  31.9 7.9 %collective-permute-start.5 = (f32[96,512]{1,0:T(8,128)S(1)}, f32[96,512]{1,0:T(8,128)S(1)}, u32[]{:S(2)}, u32[]{:S(2)}) collective-permute-start(f32[96,512]{1,0:T(8,128)S(1)} %get-tuple-element.45), channel_id=1, source_target_pairs={{1,2},{2,1},{3,4},{4,3},{5,6},{6,5},{9,10},{10,9},{11,12},{12,11},... | collective-permute-start | bytes 589832 | tf_op jit(solution)/shard_map/ppermute | solution.py:575
  42.3 5.4 %collective-permute-start.9 = (f32[8,512]{1,0:T(8,128)S(1)}, f32[8,512]{1,0:T(8,128)S(1)}, u32[]{:S(2)}, u32[]{:S(2)}) collective-permute-start(f32[8,512]{1,0:T(8,128)S(1)} %get-tuple-element.53), channel_id=1, source_target_pairs={{1,2},{2,1},{3,4},{4,3},{5,6},{6,5},{9,10},{10,9},{11,12},{12,11},... | collective-permute-start | bytes 49160 | tf_op jit(solution)/shard_map/ppermute | solution.py:575
  45.5 2.7 %collective-permute-start.8 = (f32[8,512]{1,0:T(8,128)S(1)}, f32[8,512]{1,0:T(8,128)S(1)}, u32[]{:S(2)}, u32[]{:S(2)}) collective-permute-start(f32[8,512]{1,0:T(8,128)S(1)} %get-tuple-element.53), channel_id=1, source_target_pairs={{0,1},{1,0},{2,3},{3,2},{4,5},{5,4},{6,7},{7,6},{8,9},{9,8},{10,11... | collective-permute-start | bytes 49160 | tf_op jit(solution)/shard_map/ppermute | solution.py:575
  48.4 5.9 %collective-permute-start.12 = (f32[16,1024]{1,0:T(8,128)S(1)}, f32[16,1024]{1,0:T(8,128)S(1)}, u32[]{:S(2)}, u32[]{:S(2)}) collective-permute-start(f32[16,1024]{1,0:T(8,128)S(1)} %group_kernel.1.refs_0_), channel_id=1, source_target_pairs={{8,16},{0,24},{9,17},{1,25},{10,18},{2,26},{11,19},{3,27},{12,20},... | collective-permute-start | bytes 196616 | tf_op jit(solution)/shard_map/ppermute | solution.py:588
  51.6 2.6 %collective-permute-start.11 = (f32[16,1024]{1,0:T(8,128)S(1)}, f32[16,1024]{1,0:T(8,128)S(1)}, u32[]{:S(2)}, u32[]{:S(2)}) collective-permute-start(f32[16,1024]{1,0:T(8,128)S(1)} %group_kernel.1.refs_0_), channel_id=1, source_target_pairs={{0,16},{8,24},{1,17},{9,25},{2,18},{10,26},{3,19},{11,27},{4,20},{... | collective-permute-start | bytes 196616 | tf_op jit(solution)/shard_map/ppermute | solution.py:588
  52.9 3.7 %collective-permute-start.10 = (f32[16,1024]{1,0:T(8,128)S(1)}, f32[16,1024]{1,0:T(8,128)S(1)}, u32[]{:S(2)}, u32[]{:S(2)}) collective-permute-start(f32[16,1024]{1,0:T(8,128)S(1)} %group_kernel.1.refs_0_), channel_id=1, source_target_pairs={{0,8},{16,24},{1,9},{17,25},{2,10},{18,26},{3,11},{19,27},{4,12},{... | collective-permute-start | bytes 196616 | tf_op jit(solution)/shard_map/ppermute | solution.py:588

commit v3 on v2

--- a/solution.py
+++ b/solution.py
@@ -611,7 +611,10 @@
         x1, first, second, last, rf, c, nb, halo, inverse, step, coarse, lift, spread, ends
     ) = call(
         functools.partial(start_kernel, nodes, peers),
-        (f, coefficient.reshape(1, elements), neighbours, halo_faces) + small,
+        tuple(
+            pltpu.with_memory_space_constraint(v, pltpu.HBM)
+            for v in (f, coefficient.reshape(1, elements), neighbours, halo_faces) + small
+        ),
         (
             field, face, face, plane, ((nc, elements), F32), ((1, elements), F32), (neighbours.shape, jnp.int32),
             (halo_faces.shape, jnp.int32), ((2, n, n), BF16), ((2, 2 * n, n), BF16), ((2, 3 * nc + nodes.nf, n), BF16),

time: 59.6 us -> 52 us (0.87)
  local copies, waits for them, and re-layouts: 7.59 us -> 0 us
    unnamed x20 -> x0, local copies, waits for them, and re-layouts: 7.59 us -> none
  transfers between devices with their start and end apart: 13 -> 13, of which waited for: 5 -> 5; matrix products, arithmetic and copies ran while one was open for 0% -> 0% of each run, Pallas kernels for 16% -> 18%
where the time goes in v3:
time: 52 us; the launch traced here: 51.2 us
  starting transfers between devices  25.7 us (49%)
  Pallas kernels  19.1 us (37%)
  waiting for transfers between devices  6.05 us (12%)
    pallas_call x7, Pallas kernels, call(): pl.pallas_call(kernel, out_shape=[jax.ShapeDtypeStruct(shape, dtype) for...  19.1 us
    ppermute x6, starting transfers between devices, swapped(): return [lax.ppermute(v, 'space', q) for v, q in zip((first, second), pairs)]  11.2 us
    ppermute x4, starting transfers between devices, handed_on(): lax.ppermute(last, 'slab', [(i, i + 1) for i in range(k, peers - 1, 2)])  8.67 us
    ppermute x3, starting transfers between devices, earlier(): lax.ppermute(mine, 'slab', [(a, b) for a, b in pairs if 0 <= a < b])  5.85 us
    ppermute x6, waiting for transfers between devices, swapped(): return [lax.ppermute(v, 'space', q) for v, q in zip((first, second), pairs)]  3.64 us
    ppermute x3, waiting for transfers between devices, earlier(): lax.ppermute(mine, 'slab', [(a, b) for a, b in pairs if 0 <= a < b])  2.39 us
  transfers between devices with their start and end apart: 13, of which 5 were waited for; matrix products, arithmetic and copies ran while one was open for 0% of the time, Pallas kernels for 18%

profile of v3, /device:TPU:9, one launch (start us, length us, event | category | flops | bytes accessed | tf_op | source)
XLA Modules:
  0.0 51.2 jit_solution(17710318264387022415)
XLA Ops:
  0.0 3.2 %start_kernel.1 = (f32[8,384,128]{2,1,0:T(8,128)S(1)}, f32[96,512]{1,0:T(8,128)S(1)}, f32[96,512]{1,0:T(8,128)S(1)}, f32[64,1024]{1,0:T(8,128)S(1)}, f32[8,1024]...) custom-call(f32[96,32,128]{2,1,0:T(8,128)} %bitcast.11, ...), custom_call_target="tpu_custom_call" | custom-call | tf_op jit(solution)/shard_map/start_kernel/pallas_call | solution.py:559
  3.2 3.7 %collective-permute-start.3 = (f32[64,1024]{1,0:T(8,128)S(1)}, f32[64,1024]{1,0:T(8,128)S(1)}, u32[]{:S(2)}, u32[]{:S(2)}) collective-permute-start(f32[64,1024]{1,0:T(8,128)S(1)} %get-tuple-element.38), channel_id=1, source_target_pairs={{8,16},{9,17},{10,18},{11,19},{12,20},{13,21},{14,22},{15,23}} | collective-permute-start | bytes 786440 | tf_op jit(solution)/shard_map/ppermute | solution.py:580
  6.9 1.3 %collective-permute-start.2 = (f32[64,1024]{1,0:T(8,128)S(1)}, f32[64,1024]{1,0:T(8,128)S(1)}, u32[]{:S(2)}, u32[]{:S(2)}) collective-permute-start(f32[64,1024]{1,0:T(8,128)S(1)} %get-tuple-element.38), channel_id=1, source_target_pairs={{0,8},{16,24},{1,9},{17,25},{2,10},{18,26},{3,11},{19,27},{4,12},{... | collective-permute-start | bytes 786440 | tf_op jit(solution)/shard_map/ppermute | solution.py:580
  8.2 1.3 %collective-permute-start = (f32[96,512]{1,0:T(8,128)S(1)}, f32[96,512]{1,0:T(8,128)S(1)}, u32[]{:S(2)}, u32[]{:S(2)}) collective-permute-start(f32[96,512]{1,0:T(8,128)S(1)} %get-tuple-element.36), channel_id=1, source_target_pairs={{0,1},{1,0},{2,3},{3,2},{4,5},{5,4},{6,7},{7,6},{8,9},{9,8},{10,11... | collective-permute-start | bytes 589832 | tf_op jit(solution)/shard_map/ppermute | solution.py:575
  9.5 2.0 %collective-permute-start.1 = (f32[96,512]{1,0:T(8,128)S(1)}, f32[96,512]{1,0:T(8,128)S(1)}, u32[]{:S(2)}, u32[]{:S(2)}) collective-permute-start(f32[96,512]{1,0:T(8,128)S(1)} %get-tuple-element.37), channel_id=1, source_target_pairs={{1,2},{2,1},{3,4},{4,3},{5,6},{6,5},{9,10},{10,9},{11,12},{12,11},... | collective-permute-start | bytes 589832 | tf_op jit(solution)/shard_map/ppermute | solution.py:575
  11.5 4.7 %local_kernel.2 = (f32[8,384,128]{2,1,0:T(8,128)S(1)}, f32[8,384,128]{2,1,0:T(8,128)S(1)}) custom-call(f32[8,384,128]{2,1,0:T(8,128)S(1)} %get-tuple-element.30.x_ref.x1_ref, f32[8,384,128]{2,1,0:T(8,128)S(1)} %get-tuple-element.30.x_ref.x1_ref, f32[1,1024]{1,0:T(1,128)S(1)} %get-tuple-element.31.c_ref, s32[6,1024]{1,0:T(8,128)S(1)} %get-tuple-element.32.nb_ref, ...), custom_call_target="tpu_custom_call" | custom-call | tf_op jit(solution)/shard_map/local_kernel/pallas_call | solution.py:559
  16.3 1.1 %collective-permute-done.1.got_second = f32[96,512]{1,0:T(8,128)S(1)} collective-permute-done((f32[96,512]{1,0:T(8,128)S(1)}, f32[96,512]{1,0:T(8,128)S(1)}, u32[]{:S(2)}, u32[]{:S(2)}) %collective-permute-start.1) | collective-permute-done | bytes 196640 | tf_op jit(solution)/shard_map/ppermute | solution.py:575
  17.4 2.1 %finish_kernel.1 = (f32[8,384,128]{2,1,0:T(8,128)S(1)}, f32[96,512]{1,0:T(8,128)S(1)}, f32[96,512]{1,0:T(8,128)S(1)}, f32[64,1024]{1,0:T(8,128)S(1)}) custom-call(f32[8,384,128]{2,1,0:T(8,128)S(1)} %get-tuple-element.34.base_ref, f32[8,384,128]{2,1,0:T(8,128)S(1)} %get-tuple-element.35.g_ref, f32[96,512]{1,0:T(8,128)S(1)} %collective-permute-done.got_first, ...), custom_call_target="tpu_custom_call" | custom-call | tf_op jit(solution)/shard_map/finish_kernel/pallas_call | solution.py:559
  19.5 2.4 %collective-permute-start.7 = (f32[64,1024]{1,0:T(8,128)S(1)}, f32[64,1024]{1,0:T(8,128)S(1)}, u32[]{:S(2)}, u32[]{:S(2)}) collective-permute-start(f32[64,1024]{1,0:T(8,128)S(1)} %get-tuple-element.46), channel_id=1, source_target_pairs={{8,16},{9,17},{10,18},{11,19},{12,20},{13,21},{14,22},{15,23}} | collective-permute-start | bytes 786440 | tf_op jit(solution)/shard_map/ppermute | solution.py:580
  21.9 1.3 %collective-permute-start.6 = (f32[64,1024]{1,0:T(8,128)S(1)}, f32[64,1024]{1,0:T(8,128)S(1)}, u32[]{:S(2)}, u32[]{:S(2)}) collective-permute-start(f32[64,1024]{1,0:T(8,128)S(1)} %get-tuple-element.46), channel_id=1, source_target_pairs={{0,8},{16,24},{1,9},{17,25},{2,10},{18,26},{3,11},{19,27},{4,12},{... | collective-permute-start | bytes 786440 | tf_op jit(solution)/shard_map/ppermute | solution.py:580
  23.2 1.3 %collective-permute-start.4 = (f32[96,512]{1,0:T(8,128)S(1)}, f32[96,512]{1,0:T(8,128)S(1)}, u32[]{:S(2)}, u32[]{:S(2)}) collective-permute-start(f32[96,512]{1,0:T(8,128)S(1)} %get-tuple-element.44), channel_id=1, source_target_pairs={{0,1},{1,0},{2,3},{3,2},{4,5},{5,4},{6,7},{7,6},{8,9},{9,8},{10,11... | collective-permute-start | bytes 589832 | tf_op jit(solution)/shard_map/ppermute | solution.py:575
  24.6 2.1 %collective-permute-start.5 = (f32[96,512]{1,0:T(8,128)S(1)}, f32[96,512]{1,0:T(8,128)S(1)}, u32[]{:S(2)}, u32[]{:S(2)}) collective-permute-start(f32[96,512]{1,0:T(8,128)S(1)} %get-tuple-element.45), channel_id=1, source_target_pairs={{1,2},{2,1},{3,4},{4,3},{5,6},{6,5},{9,10},{10,9},{11,12},{12,11},... | collective-permute-start | bytes 589832 | tf_op jit(solution)/shard_map/ppermute | solution.py:575
  26.6 4.7 %local_kernel.3 = (f32[8,384,128]{2,1,0:T(8,128)S(1)}, f32[8,384,128]{2,1,0:T(8,128)S(1)}) custom-call(f32[8,384,128]{2,1,0:T(8,128)S(1)} %get-tuple-element.41.x_ref, f32[8,384,128]{2,1,0:T(8,128)S(1)} %get-tuple-element.30.x_ref.x1_ref, f32[1,1024]{1,0:T(1,128)S(1)} %get-tuple-element.31.c_ref, s32[6,1024]{1,0:T(8,128)S(1)} %get-tuple-element.32.nb_ref, ...), custom_call_target="tpu_custom_call" | custom-call | tf_op jit(solution)/shard_map/local_kernel/pallas_call | solution.py:559
  31.4 1.1 %collective-permute-done.5.got_second = f32[96,512]{1,0:T(8,128)S(1)} collective-permute-done((f32[96,512]{1,0:T(8,128)S(1)}, f32[96,512]{1,0:T(8,128)S(1)}, u32[]{:S(2)}, u32[]{:S(2)}) %collective-permute-start.5) | collective-permute-done | bytes 196640 | tf_op jit(solution)/shard_map/ppermute | solution.py:575
  32.5 2.5 %coarse_kernel.1 = (f32[8,384,128]{2,1,0:T(8,128)S(1)}, f32[8,512]{1,0:T(8,128)S(1)}, f32[16,1024]{1,0:T(8,128)S(1)}) custom-call(f32[8,384,128]{2,1,0:T(8,128)S(1)} %get-tuple-element.42.base_ref, f32[8,384,128]{2,1,0:T(8,128)S(1)} %get-tuple-element.43.g_ref, f32[96,512]{1,0:T(8,128)S(1)} %collective-permute-done.4.got_first, ...), custom_call_target="tpu_custom_call" | custom-call | tf_op jit(solution)/shard_map/coarse_kernel/pallas_call | solution.py:559
  35.0 3.2 %collective-permute-start.9 = (f32[8,512]{1,0:T(8,128)S(1)}, f32[8,512]{1,0:T(8,128)S(1)}, u32[]{:S(2)}, u32[]{:S(2)}) collective-permute-start(f32[8,512]{1,0:T(8,128)S(1)} %get-tuple-element.53), channel_id=1, source_target_pairs={{1,2},{2,1},{3,4},{4,3},{5,6},{6,5},{9,10},{10,9},{11,12},{12,11},... | collective-permute-start | bytes 49160 | tf_op jit(solution)/shard_map/ppermute | solution.py:575
  38.2 1.3 %collective-permute-start.8 = (f32[8,512]{1,0:T(8,128)S(1)}, f32[8,512]{1,0:T(8,128)S(1)}, u32[]{:S(2)}, u32[]{:S(2)}) collective-permute-start(f32[8,512]{1,0:T(8,128)S(1)} %get-tuple-element.53), channel_id=1, source_target_pairs={{0,1},{1,0},{2,3},{3,2},{4,5},{5,4},{6,7},{7,6},{8,9},{9,8},{10,11... | collective-permute-start | bytes 49160 | tf_op jit(solution)/shard_map/ppermute | solution.py:575
  39.5 0.9 %collective-permute-done.9.got_second = f32[8,512]{1,0:T(8,128)S(1)} collective-permute-done((f32[8,512]{1,0:T(8,128)S(1)}, f32[8,512]{1,0:T(8,128)S(1)}, u32[]{:S(2)}, u32[]{:S(2)}) %collective-permute-start.9) | collective-permute-done | bytes 16416 | tf_op jit(solution)/shard_map/ppermute | solution.py:575
  40.4 0.5 collective-permute-done.8.got_first
  41.0 3.3 %collective-permute-start.12 = (f32[16,1024]{1,0:T(8,128)S(1)}, f32[16,1024]{1,0:T(8,128)S(1)}, u32[]{:S(2)}, u32[]{:S(2)}) collective-permute-start(f32[16,1024]{1,0:T(8,128)S(1)} %group_kernel.1.refs_0_), channel_id=1, source_target_pairs={{8,16},{0,24},{9,17},{1,25},{10,18},{2,26},{11,19},{3,27},{12,20},... | collective-permute-start | bytes 196616 | tf_op jit(solution)/shard_map/ppermute | solution.py:588
  44.3 1.3 %collective-permute-start.11 = (f32[16,1024]{1,0:T(8,128)S(1)}, f32[16,1024]{1,0:T(8,128)S(1)}, u32[]{:S(2)}, u32[]{:S(2)}) collective-permute-start(f32[16,1024]{1,0:T(8,128)S(1)} %group_kernel.1.refs_0_), channel_id=1, source_target_pairs={{0,16},{8,24},{1,17},{9,25},{2,18},{10,26},{3,19},{11,27},{4,20},{... | collective-permute-start | bytes 196616 | tf_op jit(solution)/shard_map/ppermute | solution.py:588
  45.6 1.3 %collective-permute-start.10 = (f32[16,1024]{1,0:T(8,128)S(1)}, f32[16,1024]{1,0:T(8,128)S(1)}, u32[]{:S(2)}, u32[]{:S(2)}) collective-permute-start(f32[16,1024]{1,0:T(8,128)S(1)} %group_kernel.1.refs_0_), channel_id=1, source_target_pairs={{0,8},{16,24},{1,9},{17,25},{2,10},{18,26},{3,11},{19,27},{4,12},{... | collective-permute-start | bytes 196616 | tf_op jit(solution)/shard_map/ppermute | solution.py:588
  46.9 2.4 %collective-permute-done.10.refs_1_ = f32[16,1024]{1,0:T(8,128)S(1)} collective-permute-done((f32[16,1024]{1,0:T(8,128)S(1)}, f32[16,1024]{1,0:T(8,128)S(1)}, u32[]{:S(2)}, u32[]{:S(2)}) %collective-permute-start.10) | collective-permute-done | bytes 65568 | tf_op jit(solution)/shard_map/ppermute | solution.py:588
  49.3 1.7 %end_kernel.1 = f32[96,32,128]{2,1,0:T(8,128)} custom-call(f32[8,384,128]{2,1,0:T(8,128)S(1)} %get-tuple-element.50.x_ref, bf16[2,192,64]{2,1,0:T(8,128)(2,1)S(1)} %get-tuple-element.51.lift_ref, f32[16,1024]{1,0:T(8,128)S(1)} %group_kernel.1.refs_0_, f32[16,1024]{1,0:T(8,128)S(1)} %collective-permute-done.10.refs_1_, ...), custom_call_target="tpu_custom_call" | custom-call | tf_op jit(solution)/shard_map/end_kernel/pallas_call | solution.py:559
  (9 shorter events, 0.2 us)
Async XLA Ops:
  3.2 14.2 %collective-permute-start.3 = (f32[64,1024]{1,0:T(8,128)S(1)}, f32[64,1024]{1,0:T(8,128)S(1)}, u32[]{:S(2)}, u32[]{:S(2)}) collective-permute-start(f32[64,1024]{1,0:T(8,128)S(1)} %get-tuple-element.38), channel_id=1, source_target_pairs={{8,16},{9,17},{10,18},{11,19},{12,20},{13,21},{14,22},{15,23}} | collective-permute-start | bytes 786440 | tf_op jit(solution)/shard_map/ppermute | solution.py:580
  6.9 10.5 %collective-permute-start.2 = (f32[64,1024]{1,0:T(8,128)S(1)}, f32[64,1024]{1,0:T(8,128)S(1)}, u32[]{:S(2)}, u32[]{:S(2)}) collective-permute-start(f32[64,1024]{1,0:T(8,128)S(1)} %get-tuple-element.38), channel_id=1, source_target_pairs={{0,8},{16,24},{1,9},{17,25},{2,10},{18,26},{3,11},{19,27},{4,12},{... | collective-permute-start | bytes 786440 | tf_op jit(solution)/shard_map/ppermute | solution.py:580
  8.2 8.1 %collective-permute-start = (f32[96,512]{1,0:T(8,128)S(1)}, f32[96,512]{1,0:T(8,128)S(1)}, u32[]{:S(2)}, u32[]{:S(2)}) collective-permute-start(f32[96,512]{1,0:T(8,128)S(1)} %get-tuple-element.36), channel_id=1, source_target_pairs={{0,1},{1,0},{2,3},{3,2},{4,5},{5,4},{6,7},{7,6},{8,9},{9,8},{10,11... | collective-permute-start | bytes 589832 | tf_op jit(solution)/shard_map/ppermute | solution.py:575
  9.5 7.9 %collective-permute-start.1 = (f32[96,512]{1,0:T(8,128)S(1)}, f32[96,512]{1,0:T(8,128)S(1)}, u32[]{:S(2)}, u32[]{:S(2)}) collective-permute-start(f32[96,512]{1,0:T(8,128)S(1)} %get-tuple-element.37), channel_id=1, source_target_pairs={{1,2},{2,1},{3,4},{4,3},{5,6},{6,5},{9,10},{10,9},{11,12},{12,11},... | collective-permute-start | bytes 589832 | tf_op jit(solution)/shard_map/ppermute | solution.py:575
  19.5 12.9 %collective-permute-start.7 = (f32[64,1024]{1,0:T(8,128)S(1)}, f32[64,1024]{1,0:T(8,128)S(1)}, u32[]{:S(2)}, u32[]{:S(2)}) collective-permute-start(f32[64,1024]{1,0:T(8,128)S(1)} %get-tuple-element.46), channel_id=1, source_target_pairs={{8,16},{9,17},{10,18},{11,19},{12,20},{13,21},{14,22},{15,23}} | collective-permute-start | bytes 786440 | tf_op jit(solution)/shard_map/ppermute | solution.py:580
  21.9 10.5 %collective-permute-start.6 = (f32[64,1024]{1,0:T(8,128)S(1)}, f32[64,1024]{1,0:T(8,128)S(1)}, u32[]{:S(2)}, u32[]{:S(2)}) collective-permute-start(f32[64,1024]{1,0:T(8,128)S(1)} %get-tuple-element.46), channel_id=1, source_target_pairs={{0,8},{16,24},{1,9},{17,25},{2,10},{18,26},{3,11},{19,27},{4,12},{... | collective-permute-start | bytes 786440 | tf_op jit(solution)/shard_map/ppermute | solution.py:580
  23.2 8.1 %collective-permute-start.4 = (f32[96,512]{1,0:T(8,128)S(1)}, f32[96,512]{1,0:T(8,128)S(1)}, u32[]{:S(2)}, u32[]{:S(2)}) collective-permute-start(f32[96,512]{1,0:T(8,128)S(1)} %get-tuple-element.44), channel_id=1, source_target_pairs={{0,1},{1,0},{2,3},{3,2},{4,5},{5,4},{6,7},{7,6},{8,9},{9,8},{10,11... | collective-permute-start | bytes 589832 | tf_op jit(solution)/shard_map/ppermute | solution.py:575
  24.6 7.9 %collective-permute-start.5 = (f32[96,512]{1,0:T(8,128)S(1)}, f32[96,512]{1,0:T(8,128)S(1)}, u32[]{:S(2)}, u32[]{:S(2)}) collective-permute-start(f32[96,512]{1,0:T(8,128)S(1)} %get-tuple-element.45), channel_id=1, source_target_pairs={{1,2},{2,1},{3,4},{4,3},{5,6},{6,5},{9,10},{10,9},{11,12},{12,11},... | collective-permute-start | bytes 589832 | tf_op jit(solution)/shard_map/ppermute | solution.py:575
  35.0 5.4 %collective-permute-start.9 = (f32[8,512]{1,0:T(8,128)S(1)}, f32[8,512]{1,0:T(8,128)S(1)}, u32[]{:S(2)}, u32[]{:S(2)}) collective-permute-start(f32[8,512]{1,0:T(8,128)S(1)} %get-tuple-element.53), channel_id=1, source_target_pairs={{1,2},{2,1},{3,4},{4,3},{5,6},{6,5},{9,10},{10,9},{11,12},{12,11},... | collective-permute-start | bytes 49160 | tf_op jit(solution)/shard_map/ppermute | solution.py:575
  38.2 2.7 %collective-permute-start.8 = (f32[8,512]{1,0:T(8,128)S(1)}, f32[8,512]{1,0:T(8,128)S(1)}, u32[]{:S(2)}, u32[]{:S(2)}) collective-permute-start(f32[8,512]{1,0:T(8,128)S(1)} %get-tuple-element.53), channel_id=1, source_target_pairs={{0,1},{1,0},{2,3},{3,2},{4,5},{5,4},{6,7},{7,6},{8,9},{9,8},{10,11... | collective-permute-start | bytes 49160 | tf_op jit(solution)/shard_map/ppermute | solution.py:575
  41.0 5.9 %collective-permute-start.12 = (f32[16,1024]{1,0:T(8,128)S(1)}, f32[16,1024]{1,0:T(8,128)S(1)}, u32[]{:S(2)}, u32[]{:S(2)}) collective-permute-start(f32[16,1024]{1,0:T(8,128)S(1)} %group_kernel.1.refs_0_), channel_id=1, source_target_pairs={{8,16},{0,24},{9,17},{1,25},{10,18},{2,26},{11,19},{3,27},{12,20},... | collective-permute-start | bytes 196616 | tf_op jit(solution)/shard_map/ppermute | solution.py:588
  44.3 2.6 %collective-permute-start.11 = (f32[16,1024]{1,0:T(8,128)S(1)}, f32[16,1024]{1,0:T(8,128)S(1)}, u32[]{:S(2)}, u32[]{:S(2)}) collective-permute-start(f32[16,1024]{1,0:T(8,128)S(1)} %group_kernel.1.refs_0_), channel_id=1, source_target_pairs={{0,16},{8,24},{1,17},{9,25},{2,18},{10,26},{3,19},{11,27},{4,20},{... | collective-permute-start | bytes 196616 | tf_op jit(solution)/shard_map/ppermute | solution.py:588
  45.6 3.7 %collective-permute-start.10 = (f32[16,1024]{1,0:T(8,128)S(1)}, f32[16,1024]{1,0:T(8,128)S(1)}, u32[]{:S(2)}, u32[]{:S(2)}) collective-permute-start(f32[16,1024]{1,0:T(8,128)S(1)} %group_kernel.1.refs_0_), channel_id=1, source_target_pairs={{0,8},{16,24},{1,9},{17,25},{2,10},{18,26},{3,11},{19,27},{4,12},{... | collective-permute-start | bytes 196616 | tf_op jit(solution)/shard_map/ppermute | solution.py:588
